TPU v7x, 32 devices: a whole 2x2x4 slice. The times are simulated.
32 devices in a mesh: rep: 8 (over z, y), grp: 4 (over x, core).
Axes of the slice: x: 2, y: 2, z: 4, core: 2. Of those that a mesh axis runs over, the one named last changes fastest.
Arguments:
- layer_input: bfloat16 [8, 1536, 1024], P('rep', 'grp'), may hold values from -4 to 4
- branch: int32 [8, 2], P('rep'), may hold values from 192 to 768, as said below
- attention_gain: bfloat16 [1024], P('grp'), may hold values from 0.5 to 1.5
- factor_weight: bfloat16 [1024, 800], P('grp'), may hold values from -0.3125 to 0.3125
- output_weight: bfloat16 [1024, 1024], P('grp'), may hold values from -0.375 to 0.375
- feed_gain: bfloat16 [1024], P('grp'), may hold values from 0.5 to 1.5
- gate_weight: bfloat16 [1024, 2816], P('grp'), may hold values from -0.1875 to 0.1875
- up_weight: bfloat16 [1024, 2816], P('grp'), may hold values from -0.1875 to 0.1875
- down_weight: bfloat16 [2816, 1024], P('grp'), may hold values from -0.109375 to 0.109375
- cotangent: bfloat16 [8, 1536, 1024], P('rep', 'grp'), may hold values from -4 to 4
Outputs:
- layer_output: bfloat16 [8, 1536, 1024], P('rep', 'grp')
- input_grad: float32 [8, 1536, 1024], P('rep', 'grp')
- attention_gain_grad: float32 [1024], P('grp')
- factor_weight_grad: float32 [1024, 800], P('grp')
- output_weight_grad: float32 [1024, 1024], P('grp')
- feed_gain_grad: float32 [1024], P('grp')
- gate_weight_grad: float32 [1024, 2816], P('grp')
- up_weight_grad: float32 [1024, 2816], P('grp')
- down_weight_grad: float32 [2816, 1024], P('grp')
Inputs may be any that keep to these rules, and one draw needn't show every extreme that they name: Continuation c of group g follows the first branch[g, c] prompt tokens; in every group one continuation follows all 768.
All inputs are finite; a program needn't handle non-finite values.
Results may differ from a plain program's by a relative error of at most 0.024.
The roundings to bfloat16 on the way count: a program that leaves them out, or rounds other values in their place, can miss the bound.
Values may be sent and summed in bfloat16 or wider, within the bound.
No kernel may reach another device: no remote copies, remote signals or barrier semaphores. Data moves between devices by JAX's collectives and lax.ppermute only.
A program may use at most 128 MiB of HBM per device.

v0:
```python
import jax
import jax.numpy as jnp
from jax import lax
from jax.sharding import PartitionSpec as P

HEADS = 16
HDIM = 64
QRANK = 6
KRANK = 2


highest = lax.Precision.HIGHEST


def rms_scale(values):
    return lax.rsqrt(jnp.mean(values * values, axis=-1, keepdims=True) + 1e-05)


def angles(positions, half_width):
    freqs = 10000.0 ** (-jnp.arange(half_width).astype(jnp.float32) / half_width)
    phase = positions.astype(jnp.float32)[:, None] * freqs[None, :]
    return (jnp.cos(phase), jnp.sin(phase))


def rotate(matrix, cosine, sine, ranks):
    half_cols = matrix.shape[1] // (2 * ranks)
    pieces = matrix.reshape(matrix.shape[0], ranks, 2, half_cols)
    first_half = pieces[:, :, 0]
    second_half = pieces[:, :, 1]
    cos_wide = cosine[:, None, :]
    sin_wide = sine[:, None, :]
    turned = jnp.stack(
        [
            first_half * cos_wide - second_half * sin_wide,
            second_half * cos_wide + first_half * sin_wide,
        ],
        axis=2,
    )
    return turned.reshape(matrix.shape)


def cut_points():
    first_cut = QRANK * HEADS
    second_cut = first_cut + QRANK * HDIM
    third_cut = second_cut + KRANK * HEADS
    fourth_cut = third_cut + KRANK * HDIM
    fifth_cut = fourth_cut + KRANK * HEADS
    return (first_cut, second_cut, third_cut, fourth_cut, fifth_cut)


def turn_factors(values, cosine, sine):
    cuts = cut_points()
    return jnp.concatenate(
        [
            values[:, : cuts[0]],
            rotate(values[:, cuts[0] : cuts[1]], cosine, sine, QRANK),
            values[:, cuts[1] : cuts[2]],
            rotate(values[:, cuts[2] : cuts[3]], cosine, sine, KRANK),
            values[:, cuts[3] :],
        ],
        axis=1,
    )


def expand(head_part, dim_part, ranks, head_low, head_high):
    tokens_here = head_part.shape[0]
    left_factor = head_part.reshape(tokens_here, ranks, HEADS)[:, :, head_low:head_high]
    right_factor = dim_part.reshape(tokens_here, ranks, HDIM)
    return (
        jnp.einsum("nrh,nrd->nhd", left_factor, right_factor, preferred_element_type=jnp.float32)
        / ranks
    )


def pair_grads(head_part, dim_part, grad_heads, ranks, head_low, head_high):
    tokens_here = head_part.shape[0]
    left_factor = head_part.reshape(tokens_here, ranks, HEADS)[:, :, head_low:head_high].astype(
        jnp.float32
    )
    right_factor = dim_part.reshape(tokens_here, ranks, HDIM).astype(jnp.float32)
    left_grad = jnp.einsum("nhd,nrd->nrh", grad_heads, right_factor, precision=highest) / ranks
    left_grad = jnp.pad(left_grad, ((0, 0), (0, 0), (head_low, HEADS - head_high)))
    right_grad = jnp.einsum("nhd,nrh->nrd", grad_heads, left_factor, precision=highest) / ranks
    return (
        left_grad.reshape(tokens_here, ranks * HEADS),
        right_grad.reshape(tokens_here, ranks * HDIM),
    )


def geometry(index, table, local_rows, prompt_len):
    cont_count = table.shape[0]
    inside = index < prompt_len
    segment = jnp.where(inside, -1, (index - prompt_len) // local_rows)
    chosen = jnp.sum(
        jnp.where(jnp.arange(cont_count)[None, :] == segment[:, None], table[None, :], 0), axis=1
    )
    position = jnp.where(inside, index, chosen + (index - prompt_len) % local_rows)
    limit = jnp.where(inside, 0, chosen)
    return (segment, position, limit)


def keep_state(state):
    return state


def norm_back(grad_hidden, normed, scale, gain_vector):
    grad_normed = grad_hidden * gain_vector
    gain_grad = jnp.sum(grad_hidden * normed, axis=0)
    grad_values = scale * (
        grad_normed - normed * jnp.mean(grad_normed * normed, axis=-1, keepdims=True)
    )
    return (gain_grad, grad_values)


def local(
    layer_input,
    branch,
    attention_gain,
    factor_weight,
    output_weight,
    feed_gain,
    gate_weight,
    up_weight,
    down_weight,
    cotangent,
):
    gathered = (
        lax.all_gather(attention_gain, "grp", axis=0, tiled=True),
        lax.all_gather(factor_weight, "grp", axis=0, tiled=True),
        lax.all_gather(output_weight, "grp", axis=0, tiled=True),
        lax.all_gather(feed_gain, "grp", axis=0, tiled=True),
        lax.all_gather(gate_weight, "grp", axis=0, tiled=True),
        lax.all_gather(up_weight, "grp", axis=0, tiled=True),
        lax.all_gather(down_weight, "grp", axis=0, tiled=True),
    )
    local_rows = layer_input.shape[1]
    shard_count = lax.axis_size("grp")
    shard_place = lax.axis_index("grp")
    prompt_len = local_rows * (shard_count // 2)
    token_total = local_rows * shard_count
    query_index = shard_place * local_rows + jnp.arange(local_rows, dtype=jnp.int32)
    query_seg, query_pos, query_lim = geometry(query_index, branch[0], local_rows, prompt_len)
    cuts = cut_points()
    offsets = (cuts[2] - cuts[1], cuts[3] - cuts[1], cuts[4] - cuts[1])
    residual_in = layer_input[0].astype(jnp.float32)
    scale_one = rms_scale(residual_in)
    normed_one = residual_in * scale_one
    gain_one = gathered[0].astype(jnp.float32)
    hidden_one = (normed_one * gain_one).astype(jnp.bfloat16)
    raw_factors = jnp.dot(hidden_one, gathered[1], preferred_element_type=jnp.float32)
    cosine, sine = angles(query_pos, HDIM // 2)
    factors = turn_factors(raw_factors, cosine, sine).astype(jnp.bfloat16)
    key_table = lax.all_gather(factors[:, cuts[1] :], "grp", axis=0, tiled=True)
    table_cols = key_table.shape[1]
    queries = expand(factors[:, : cuts[0]], factors[:, cuts[0] : cuts[1]], QRANK, 0, HEADS).astype(
        jnp.bfloat16
    )
    block_rows = 512
    block_count = token_total // block_rows
    head_span = HEADS // 2
    block_numbers = jnp.arange(block_count)

    def visible(number):
        key_index = number * block_rows + jnp.arange(block_rows, dtype=jnp.int32)
        key_seg = jnp.where(key_index < prompt_len, -1, (key_index - prompt_len) // local_rows)
        same_line = (key_seg[None, :] == query_seg[:, None]) & (
            key_index[None, :] <= query_index[:, None]
        )
        from_prompt = (key_seg[None, :] == -1) & (key_index[None, :] < query_lim[:, None])
        return same_line | from_prompt

    def key_values(number, head_low, head_high):
        key_piece = lax.dynamic_slice_in_dim(key_table, number * block_rows, block_rows, 0)
        keys_now = expand(
            key_piece[:, : offsets[0]],
            key_piece[:, offsets[0] : offsets[1]],
            KRANK,
            head_low,
            head_high,
        ).astype(jnp.bfloat16)
        values_now = expand(
            key_piece[:, offsets[1] : offsets[2]],
            key_piece[:, offsets[2] :],
            KRANK,
            head_low,
            head_high,
        ).astype(jnp.bfloat16)
        return (key_piece, keys_now, values_now)

    def scores(query_half, keys_now, visible_now):
        logits = jnp.einsum(
            "qhd,khd->hqk", query_half, keys_now, preferred_element_type=jnp.float32
        ) * HDIM ** (-0.5)
        return jnp.where(visible_now[None], logits, -1e30)

    def half_forward(head_low, head_high):
        query_half = queries[:, head_low:head_high]

        def totals_step(carry, number):
            visible_now = visible(number)

            def totals_update(state):
                running_top, running_mass = state
                _, keys_now, _ = key_values(number, head_low, head_high)
                logits = scores(query_half, keys_now, visible_now)
                new_top = jnp.maximum(running_top, jnp.max(logits, axis=-1))
                new_mass = running_mass * jnp.exp(running_top - new_top) + jnp.sum(
                    jnp.exp(logits - new_top[..., None]), axis=-1
                )
                return (new_top, new_mass)

            return (lax.cond(jnp.any(visible_now), totals_update, keep_state, carry), None)

        start_state = (
            jnp.full((head_span, local_rows), -1e30, jnp.float32),
            jnp.zeros((head_span, local_rows), jnp.float32),
        )
        (final_top, final_mass), _ = lax.scan(totals_step, start_state, block_numbers)
        log_total = final_top + jnp.log(final_mass)

        def output_step(carry, number):
            visible_now = visible(number)

            def output_update(state):
                main_sum, rest_sum = state
                _, keys_now, values_now = key_values(number, head_low, head_high)
                probs = jnp.exp(scores(query_half, keys_now, visible_now) - log_total[..., None])
                probs_low = probs.astype(jnp.bfloat16)
                probs_rest = (probs - probs_low.astype(jnp.float32)).astype(jnp.bfloat16)
                main_sum = main_sum + jnp.einsum(
                    "hqk,khd->qhd", probs_low, values_now, preferred_element_type=jnp.float32
                )
                rest_sum = rest_sum + jnp.einsum(
                    "hqk,khd->qhd", probs_rest, values_now, preferred_element_type=jnp.float32
                )
                return (main_sum, rest_sum)

            return (lax.cond(jnp.any(visible_now), output_update, keep_state, carry), None)

        zero_out = jnp.zeros((local_rows, head_span, HDIM), jnp.float32)
        (main_sum, rest_sum), _ = lax.scan(output_step, (zero_out, zero_out), block_numbers)
        return (log_total, main_sum, main_sum + rest_sum)

    first_pass = half_forward(0, head_span)
    second_pass = half_forward(head_span, HEADS)
    attended = (
        jnp.concatenate([first_pass[1], second_pass[1]], axis=1)
        .reshape(local_rows, HEADS * HDIM)
        .astype(jnp.bfloat16)
    )
    middle = residual_in + jnp.dot(attended, gathered[2], preferred_element_type=jnp.float32)
    scale_two = rms_scale(middle)
    normed_two = middle * scale_two
    gain_two = gathered[3].astype(jnp.float32)
    hidden_two = (normed_two * gain_two).astype(jnp.bfloat16)
    gate_values = jnp.dot(hidden_two, gathered[4], preferred_element_type=jnp.float32)
    up_values = jnp.dot(hidden_two, gathered[5], preferred_element_type=jnp.float32)
    sigmoid_gate = jax.nn.sigmoid(gate_values)
    active = (gate_values * sigmoid_gate * up_values).astype(jnp.bfloat16)
    result = middle + jnp.dot(active, gathered[6], preferred_element_type=jnp.float32)
    upstream = cotangent[0]
    down_grad = jnp.einsum("tf,td->fd", active, upstream, preferred_element_type=jnp.float32)
    active_grad = jnp.einsum("td,fd->tf", upstream, gathered[6], preferred_element_type=jnp.float32)
    gate_grad = (
        active_grad * up_values * sigmoid_gate * (1.0 + gate_values * (1.0 - sigmoid_gate))
    ).astype(jnp.bfloat16)
    up_grad = (active_grad * gate_values * sigmoid_gate).astype(jnp.bfloat16)
    gate_weight_grad = jnp.einsum(
        "td,tf->df", hidden_two, gate_grad, preferred_element_type=jnp.float32
    )
    up_weight_grad = jnp.einsum(
        "td,tf->df", hidden_two, up_grad, preferred_element_type=jnp.float32
    )
    hidden_two_grad = jnp.einsum(
        "tf,df->td", gate_grad, gathered[4], preferred_element_type=jnp.float32
    ) + jnp.einsum("tf,df->td", up_grad, gathered[5], preferred_element_type=jnp.float32)
    feed_gain_grad, middle_grad = norm_back(
        hidden_two_grad, normed_two, scale_two, gathered[3].astype(jnp.float32)
    )
    middle_grad = middle_grad + upstream.astype(jnp.float32)
    branch_grad = middle_grad.astype(jnp.bfloat16)
    output_weight_grad = jnp.einsum(
        "tf,td->fd", attended, branch_grad, preferred_element_type=jnp.float32
    )
    grad_heads = (
        jnp.einsum("td,fd->tf", branch_grad, gathered[2], preferred_element_type=jnp.float32)
        .astype(jnp.bfloat16)
        .reshape(local_rows, HEADS, HDIM)
    )

    def half_backward(head_low, head_high, log_total, exact_half):
        query_half = queries[:, head_low:head_high]
        grad_half = grad_heads[:, head_low:head_high]
        delta = jnp.sum(grad_half.astype(jnp.float32) * exact_half, axis=-1).T

        def grad_step(carry, number):
            visible_now = visible(number)

            def grad_update(query_grad):
                key_piece, keys_now, values_now = key_values(number, head_low, head_high)
                probs = jnp.exp(scores(query_half, keys_now, visible_now) - log_total[..., None])
                prob_grad = jnp.einsum(
                    "qhd,khd->hqk", grad_half, values_now, preferred_element_type=jnp.float32
                )
                score_grad = (probs * (prob_grad - delta[..., None])).astype(jnp.bfloat16)
                query_grad = query_grad + jnp.einsum(
                    "hqk,khd->qhd", score_grad, keys_now, preferred_element_type=jnp.float32
                ) * HDIM ** (-0.5)
                key_grad = jnp.einsum(
                    "hqk,qhd->khd", score_grad, query_half, preferred_element_type=jnp.float32
                ) * HDIM ** (-0.5)
                value_grad = jnp.einsum(
                    "hqk,qhd->khd",
                    probs.astype(jnp.bfloat16),
                    grad_half,
                    preferred_element_type=jnp.float32,
                )
                key_heads, key_dims = pair_grads(
                    key_piece[:, : offsets[0]],
                    key_piece[:, offsets[0] : offsets[1]],
                    key_grad,
                    KRANK,
                    head_low,
                    head_high,
                )
                value_heads, value_dims = pair_grads(
                    key_piece[:, offsets[1] : offsets[2]],
                    key_piece[:, offsets[2] :],
                    value_grad,
                    KRANK,
                    head_low,
                    head_high,
                )
                return (
                    query_grad,
                    jnp.concatenate([key_heads, key_dims, value_heads, value_dims], axis=1),
                )

            def skip_block(query_grad):
                return (query_grad, jnp.zeros((block_rows, table_cols), jnp.float32))

            return lax.cond(jnp.any(visible_now), grad_update, skip_block, carry)

        query_grad, table_grads = lax.scan(
            grad_step, jnp.zeros((local_rows, head_span, HDIM), jnp.float32), block_numbers
        )
        return (query_grad, table_grads.reshape(token_total, table_cols))

    first_back = half_backward(0, head_span, first_pass[0], first_pass[2])
    second_back = half_backward(head_span, HEADS, second_pass[0], second_pass[2])
    query_grad = jnp.concatenate([first_back[0], second_back[0]], axis=1)
    own_table_grad = lax.psum_scatter(
        (first_back[1] + second_back[1]).astype(jnp.bfloat16),
        "grp",
        scatter_dimension=0,
        tiled=True,
    ).astype(jnp.float32)
    query_heads, query_dims = pair_grads(
        factors[:, : cuts[0]], factors[:, cuts[0] : cuts[1]], query_grad, QRANK, 0, HEADS
    )
    factor_grad = jnp.concatenate([query_heads, query_dims, own_table_grad], axis=1)
    raw_grad = turn_factors(factor_grad, cosine, -sine).astype(jnp.bfloat16)
    factor_weight_grad = jnp.einsum(
        "td,tf->df", hidden_one, raw_grad, preferred_element_type=jnp.float32
    )
    hidden_one_grad = jnp.einsum(
        "tf,df->td", raw_grad, gathered[1], preferred_element_type=jnp.float32
    )
    attention_gain_grad, input_part = norm_back(
        hidden_one_grad, normed_one, scale_one, gathered[0].astype(jnp.float32)
    )
    input_grad = middle_grad + input_part
    shard_grads = (
        lax.psum_scatter(
            attention_gain_grad.astype(jnp.bfloat16), "grp", scatter_dimension=0, tiled=True
        ).astype(jnp.float32),
        lax.psum_scatter(
            factor_weight_grad.astype(jnp.bfloat16), "grp", scatter_dimension=0, tiled=True
        ).astype(jnp.float32),
        lax.psum_scatter(
            output_weight_grad.astype(jnp.bfloat16), "grp", scatter_dimension=0, tiled=True
        ).astype(jnp.float32),
        lax.psum_scatter(
            feed_gain_grad.astype(jnp.bfloat16), "grp", scatter_dimension=0, tiled=True
        ).astype(jnp.float32),
        lax.psum_scatter(
            gate_weight_grad.astype(jnp.bfloat16), "grp", scatter_dimension=0, tiled=True
        ).astype(jnp.float32),
        lax.psum_scatter(
            up_weight_grad.astype(jnp.bfloat16), "grp", scatter_dimension=0, tiled=True
        ).astype(jnp.float32),
        lax.psum_scatter(
            down_grad.astype(jnp.bfloat16), "grp", scatter_dimension=0, tiled=True
        ).astype(jnp.float32),
    )
    final_grads = (
        lax.psum(shard_grads[0].astype(jnp.bfloat16), "rep").astype(jnp.float32),
        lax.psum(shard_grads[1].astype(jnp.bfloat16), "rep").astype(jnp.float32),
        lax.psum(shard_grads[2].astype(jnp.bfloat16), "rep").astype(jnp.float32),
        lax.psum(shard_grads[3].astype(jnp.bfloat16), "rep").astype(jnp.float32),
        lax.psum(shard_grads[4].astype(jnp.bfloat16), "rep").astype(jnp.float32),
        lax.psum(shard_grads[5].astype(jnp.bfloat16), "rep").astype(jnp.float32),
        lax.psum(shard_grads[6].astype(jnp.bfloat16), "rep").astype(jnp.float32),
    )
    return (
        result.astype(jnp.bfloat16)[None],
        input_grad[None],
        final_grads[0],
        final_grads[1],
        final_grads[2],
        final_grads[3],
        final_grads[4],
        final_grads[5],
        final_grads[6],
    )


def solution(mesh):
    in_specs = (
        P("rep", "grp", None),
        P("rep", None),
        P("grp"),
        P("grp", None),
        P("grp", None),
        P("grp"),
        P("grp", None),
        P("grp", None),
        P("grp", None),
        P("rep", "grp", None),
    )
    out_specs = (
        P("rep", "grp", None),
        P("rep", "grp", None),
        P("grp"),
        P("grp", None),
        P("grp", None),
        P("grp"),
        P("grp", None),
        P("grp", None),
        P("grp", None),
    )
    return jax.shard_map(local, mesh=mesh, in_specs=in_specs, out_specs=out_specs, check_vma=False)
```

profile of v0, /device:TPU:0, one launch (start us, length us, event | category | flops | bytes accessed | tf_op | source)
XLA Modules:
  0.0 1226.2 jit_solution(16655373652148109157)
XLA Ops:
  10.8 6.0 all-gather
  17.1 5.4 all-gather.1
  24.0 8.5 all-gather.8.cloned.1.call-done
  35.3 10.3 all_gather.26
  49.0 14.9 %while.102 = (s32[]{:T(128)}, f32[8,384]{1,0:T(8,128)S(1)}, f32[8,384]{1,0:T(8,128)S(1)}, s32[3]{0:T(128)S(1)}, s32[384]{0:T(512)S(1)}, /*index=5*/bf16[1536,320...) while((s32[]{:T(128)}, f32[8,384]{1,0:T(8,128)S(1)}, ...), condition=%wide.region_8.9_spmd.clone.clone, body=%wide.region_2.8_spmd.clone.clone.sunk | while | flops 215309312 | bytes 15594281 | solution.py:218
  52.0 6.0 conditional.24
  66.4 35.9 %while.103 = (s32[]{:T(128)}, f32[384,8,64]{0,2,1:T(8,128)}, f32[384,8,64]{0,2,1:T(8,128)}, s32[3]{0:T(128)}, s32[384]{0:T(512)S(1)}, /*index=5*/bf16[1536,320]{...) while((s32[]{:T(128)}, f32[384,8,64]{0,2,1:T(8,128)}, ...), condition=%wide.region_13.14_spmd.clone.clone, body=%wide.region_9.13_spmd.clone.clone.sunk | while | flops 626738176 | bytes 35529648 | solution.py:241
  71.1 22.6 %conditional.25 = ((f32[384,8,64]{0,2,1:T(8,128)}, f32[384,8,64]{0,2,1:T(8,128)})) conditional(s32[]{:T(128)} %convert_element_type.413, (f32[384,8,64]{0,2,1:T(8,128)}, f32[384,8,64]{0,2,1:T(8,128)}) %tuple.365, (s32[]{:T(128)}, bf16[1536,320]{0,1:T(8,128)(2,1)}, pred[384,512]{0,1:T(8,128)(4,1)}, bf16[384,8,64]{0,2,1:T(8,128)(2,1)S(1)}, ...), branch_computations={%region_11.11_spmd, %region_12.12_spmd} | conditional | flops 625344512 | bytes 35315920 | solution.py:238
  76.7 3.7 fusion.46
  82.2 5.9 fusion.42
  88.1 5.6 fusion.43
  106.6 16.2 %while.104 = (s32[]{:T(128)}, f32[8,384]{1,0:T(8,128)S(1)}, f32[8,384]{1,0:T(8,128)S(1)}, s32[3]{0:T(128)S(1)}, s32[384]{0:T(512)S(1)}, /*index=5*/bf16[1536,320...) while((s32[]{:T(128)}, f32[8,384]{1,0:T(8,128)S(1)}, ...), condition=%wide.region_20.21_spmd.clone.clone, body=%wide.region_14.20_spmd.clone.clone.sunk | while | flops 215309312 | bytes 15594281 | solution.py:218
  109.7 7.1 conditional.26
  125.2 36.8 %while.105 = (s32[]{:T(128)}, f32[384,8,64]{0,2,1:T(8,128)}, f32[384,8,64]{0,2,1:T(8,128)}, s32[3]{0:T(128)}, s32[384]{0:T(512)S(1)}, /*index=5*/bf16[1536,320]{...) while((s32[]{:T(128)}, f32[384,8,64]{0,2,1:T(8,128)}, ...), condition=%wide.region_25.26_spmd.clone.clone, body=%wide.region_21.25_spmd.clone.clone.sunk | while | flops 626738176 | bytes 35529648 | solution.py:241
  129.5 23.6 %conditional.27 = ((f32[384,8,64]{0,2,1:T(8,128)}, f32[384,8,64]{0,2,1:T(8,128)})) conditional(s32[]{:T(128)} %convert_element_type.415, (f32[384,8,64]{0,2,1:T(8,128)}, f32[384,8,64]{0,2,1:T(8,128)}) %tuple.377, (s32[]{:T(128)}, bf16[1536,320]{0,1:T(8,128)(2,1)}, pred[384,512]{0,1:T(8,128)(4,1)}, bf16[384,8,64]{0,2,1:T(8,128)(2,1)}, ...), branch_computations={%region_23.23_spmd, %region_24.24_spmd} | conditional | flops 625344512 | bytes 35315920 | solution.py:238
  135.0 4.7 fusion.77
  141.6 5.9 fusion.73
  147.5 5.5 fusion.74
  164.5 2.9 multiply_reduce_fusion.2
  167.7 7.7 fusion.214
  175.4 7.2 fusion.215
  182.6 8.9 all-gather.16.cloned.1.call-done
  191.5 10.2 multiply_convert_fusion.22
  201.7 6.7 fusion.216
  208.4 3.2 multiply_reduce_fusion
  215.9 2.8 multiply_reduce_fusion.4
  221.7 96.9 %while.106 = (s32[]{:T(128)}, f32[384,8,64]{0,2,1:T(8,128)}, f32[3,512,320]{1,2,0:T(8,128)}, s32[3]{0:T(128)}, s32[384]{0:T(512)S(1)}, /*index=5*/bf16[1536,320]...) while((s32[]{:T(128)}, f32[384,8,64]{0,2,1:T(8,128)}, ...), condition=%wide.region_33.34_spmd.clone.clone, body=%wide.region_29.33_spmd.clone.clone.sunk | while | flops 1053885440 | bytes 72340984 | solution.py:344
  226.2 63.3 %conditional.28 = (f32[384,8,64]{0,2,1:T(8,128)}, f32[1,512,320]{1,2,0:T(8,128)}) conditional(s32[]{:T(128)} %convert_element_type.416, f32[384,8,64]{0,2,1:T(8,128)} %get-tuple-element.2557, (s32[]{:T(128)}, bf16[1536,320]{0,1:T(8,128)(2,1)}, pred[384,512]{0,1:T(8,128)(4,1)}, bf16[384,8,64]{0,2,1:T(8,128)(2,1)S(1)}, f32[8,384]{1,0:T(8,128)S(1)}, ...), branch_computations={%region_31.31_spmd, %region_32.32_spmd} | conditional | flops 1052491776 | bytes 70816016 | solution.py:342
  232.6 3.7 fusion.100
  241.5 5.3 fusion.86
  252.6 3.6 convolution_multiply_fusion.5
  259.4 3.5 convolution_multiply_fusion.4
  264.8 5.6 fusion.93
  272.4 3.6 convolution_multiply_fusion.3
  279.2 3.5 convolution_multiply_fusion.2
  285.9 3.6 fusion.98
  321.7 81.0 %while.107 = (s32[]{:T(128)}, f32[384,8,64]{0,2,1:T(8,128)}, f32[3,512,320]{1,2,0:T(8,128)}, s32[3]{0:T(128)}, s32[384]{0:T(512)S(1)}, /*index=5*/bf16[1536,320]...) while((s32[]{:T(128)}, f32[384,8,64]{0,2,1:T(8,128)}, ...), condition=%wide.region_39.40_spmd.clone.clone, body=%wide.region_35.39_spmd.clone.clone.sunk | while | flops 1053885440 | bytes 72193544 | solution.py:344
  326.0 60.0 %conditional.29 = (f32[384,8,64]{0,2,1:T(8,128)}, f32[1,512,320]{1,2,0:T(8,128)}) conditional(s32[]{:T(128)} %convert_element_type.417, f32[384,8,64]{0,2,1:T(8,128)} %get-tuple-element.2518, (s32[]{:T(128)}, bf16[1536,320]{0,1:T(8,128)(2,1)}, pred[384,512]{0,1:T(8,128)(4,1)}, bf16[384,8,64]{0,2,1:T(8,128)(2,1)}, f32[8,384]{1,0:T(8,128)S(1)}, ...), branch_computations={%region_37.37_spmd, %region_38.38_spmd} | conditional | flops 1052491776 | bytes 70668576 | solution.py:342
  331.6 4.7 fusion.120
  341.6 5.3 fusion.106
  348.6 3.1 fusion.116
  357.5 3.5 convolution_multiply_fusion.10
  363.0 5.5 fusion.113
  370.5 3.6 convolution_multiply_fusion.9
  382.3 3.6 fusion.118
  414.3 4.6 fusion.164
  421.5 5.5 fusion.151
  430.3 354.5 %reduce-scatter.7.cloned.1.call-done = bf16[384,320]{1,0:T(8,128)(2,1)} async-done(((bf16[1536,320]{1,0:T(8,128)(2,1)}), bf16[384,320]{1,0:T(8,128)(2,1)}) %reduce-scatter.7.cloned.1.call-update) | async-done | bytes 245776 | tf_op jit(solution)/shard_map/reduce_scatter | solution.py:352
  790.2 3.5 convolution_convert_fusion.4
  793.7 6.9 convolution_convert_fusion.2
  800.8 6.9 convolution_convert_fusion.1
  808.8 6.8 convolution_convert_fusion
  815.6 2.9 reduce-scatter.11.cloned.1.call-done
  818.6 31.0 %reduce-scatter.9.cloned.1.call-done = bf16[256,800]{0,1:T(8,128)(2,1)} async-done(((bf16[1024,800]{0,1:T(8,128)(2,1)}), bf16[256,800]{0,1:T(8,128)(2,1)}) %reduce-scatter.9.cloned.1.call-update) | async-done | bytes 409616 | tf_op jit(solution)/shard_map/reduce_scatter | solution.py:377
  849.6 57.3 %reduce-scatter.13.cloned.1.call-done = bf16[256,2816]{1,0:T(8,128)(2,1)} async-done(((bf16[1024,2816]{1,0:T(8,128)(2,1)}), bf16[256,2816]{1,0:T(8,128)(2,1)}) %reduce-scatter.13.cloned.1.call-update) | async-done | bytes 1441808 | tf_op jit(solution)/shard_map/reduce_scatter | solution.py:386
  906.9 57.1 %reduce-scatter.15.cloned.1.call-done = bf16[256,2816]{1,0:T(8,128)(2,1)} async-done(((bf16[1024,2816]{1,0:T(8,128)(2,1)}), bf16[256,2816]{1,0:T(8,128)(2,1)}) %reduce-scatter.15.cloned.1.call-update) | async-done | bytes 1441808 | tf_op jit(solution)/shard_map/reduce_scatter | solution.py:389
  964.0 57.3 %reduce-scatter.17.cloned.1.call-done = bf16[704,1024]{1,0:T(8,128)(2,1)} async-done(((bf16[2816,1024]{1,0:T(8,128)(2,1)}), bf16[704,1024]{1,0:T(8,128)(2,1)}) %reduce-scatter.17.cloned.1.call-update) | async-done | bytes 1441808 | tf_op jit(solution)/shard_map/reduce_scatter | solution.py:392
  1023.2 6.7 fusion.165
  1030.0 3.6 fusion.162
  1033.5 6.0 all-reduce.8
  1039.7 22.4 %all-reduce.6 = (bf16[256]{0:T(256)(128)(2,1)S(1)}, bf16[256]{0:T(256)(128)(2,1)S(1)}) all-reduce(bf16[256]{0:T(256)(128)(2,1)S(1)} %dynamic-slice.1, bf16[256]{0:T(256)(128)(2,1)S(1)} %dynamic-slice.3), channel_id=1, replica_groups=mesh['rep'=8,'grp'=4] {'rep'}, use_global_device_ids=true, to_apply=%region_44.45 | all-reduce | flops 512 | bytes 2048 | tf_op jit(solution)/shard_map/psum | solution.py:397
  1063.3 3.0 fusion.161
  1066.3 143.7 %all-reduce.11.cloned.1.call-done = (bf16[256,800]{0,1:T(8,128)(2,1)}, bf16[256,1024]{1,0:T(8,128)(2,1)}, bf16[256,2816]{1,0:T(8,128)(2,1)}, bf16[256,2816]{1,0:T(8,128)(2,1)}, bf16[704,1024]{1,0:T(8,128)(2,1)}) async-done(((bf16[256,800]{0,1:T(8,128)(2,1)}, bf16[256,1024]{1,0:T(8,128)(2,1)}, bf16[256,2816]{1,0:T(8,128)(2,1)}, bf16[256,2816]{1,0:T(8,128)(2,1)}, bf16[704,1024]{1,0:T(8,128)(2,1)}), ...) | async-done | bytes 5259280 | tf_op jit(solution)/shard_map/psum | solution.py:398
  1210.0 3.2 convert_element_type.275
  (445 shorter events, 215.6 us)
Async XLA Ops:
  7.2 25.3 %all-gather.8.cloned.1.call-start = ((), (), s32[]{:S(2)}) async-start(), calls=%async_computation.6 | async-start | bytes 2048000 | tf_op jit(solution)/shard_map/all_gather | solution.py:129
  7.9 156.5 %all-gather.10.cloned.1.call-start = ((), (), s32[]{:S(2)}) async-start(), calls=%async_computation.7 | async-start | bytes 2621440 | tf_op jit(solution)/shard_map/all_gather | solution.py:130
  8.7 2.0 copy-start.54
  8.7 2.1 copy-start.57
  8.7 8.2 copy-start.13
  8.7 159.0 %all-gather.12.cloned.1.call-start = ((), (), s32[]{:S(2)}) async-start(), calls=%async_computation.8 | async-start | bytes 7208960 | tf_op jit(solution)/shard_map/all_gather | solution.py:132
  9.4 7.7 copy-start.58
  9.4 165.9 %all-gather.14.cloned.1.call-start = ((), (), s32[]{:S(2)}) async-start(), calls=%async_computation.9 | async-start | bytes 7208960 | tf_op jit(solution)/shard_map/all_gather | solution.py:133
  10.0 181.4 %all-gather.16.cloned.1.call-start = ((), (), s32[]{:S(2)}) async-start(), calls=%async_computation.10 | async-start | bytes 7208960 | tf_op jit(solution)/shard_map/all_gather | solution.py:134
  10.6 774.2 %reduce-scatter.7.cloned.1.call-start = ((), (), s32[]{:S(2)}) async-start(), calls=%async_computation.11 | async-start | bytes 1474560 | tf_op jit(solution)/shard_map/reduce_scatter | solution.py:352
  16.8 18.2 %copy-start.44 = (f32[4,1,256]{2,1,0:T(1,128)}, f32[4,1,256]{2,1,0:T(1,128)S(1)}, u32[]{:S(2)}) copy-start(f32[4,1,256]{2,1,0:T(1,128)S(1)} %convert_element_type.281) | copy-start | bytes 12292
  17.1 17.9 %copy-start.51 = (f32[384]{0:T(512)}, f32[384]{0:T(512)S(1)}, u32[]{:S(2)}) copy-start(f32[384]{0:T(512)S(1)} %add_rsqrt_fusion.1) | copy-start | bytes 4612
  24.0 21.6 %copy-start.33 = (f32[384,32]{0,1:T(8,128)}, f32[384,32]{0,1:T(8,128)S(1)}, u32[]{:S(2)}) copy-start(f32[384,32]{0,1:T(8,128)S(1)} %get-tuple-element.1907) | copy-start | bytes 147460
  46.2 2.3 copy-start.20
  46.7 1.8 copy-start.21
  76.7 3.7 copy-start.10
  76.7 3.9 copy-start.27
  82.2 5.9 copy-start.23
  102.3 4.3 copy-start.46
  135.0 4.7 copy-start.11
  135.0 4.9 copy-start.28
  141.6 5.9 copy-start.24
  162.1 2.4 copy-start.48
  162.1 2.4 copy-start.14
  164.4 3.0 copy-start.18
  164.5 3.0 copy-start.43
  167.4 44.2 %copy-start.8 = (f32[384,1024]{1,0:T(8,128)}, f32[384,1024]{1,0:T(8,128)S(1)}, u32[]{:S(2)}) copy-start(f32[384,1024]{1,0:T(8,128)S(1)} %get-tuple-element.1913) | copy-start | bytes 4718596
  167.7 7.7 copy-start.35
  175.3 16.1 %copy-start.37 = (bf16[1,384,1024]{2,1,0:T(8,128)(2,1)S(1)}, bf16[1,384,1024]{2,1,0:T(8,128)(2,1)}, u32[]{:S(2)}) copy-start(bf16[1,384,1024]{2,1,0:T(8,128)(2,1)} %param.43) | copy-start | bytes 2359300
  201.7 6.7 copy-start.61
  201.7 6.7 copy-start.60
  201.7 6.7 copy-start.55
  208.4 3.2 copy-start.38
  211.6 2.0 copy-start.26
  218.7 3.0 copy-start.47
  232.5 3.7 copy-start.12
  232.5 4.6 copy-start.29
  318.6 3.0 copy-start.49
  331.6 5.6 copy-start.30
  356.3 6.7 copy-start.22
  370.5 6.2 copy-start.3
  405.1 2.0 copy-start.19
  406.6 412.0 %reduce-scatter.11.cloned.1.call-start = ((), (), s32[]{:S(2)}) async-start(), calls=%async_computation.13 | async-start | bytes 2621440 | tf_op jit(solution)/shard_map/reduce_scatter | solution.py:380
  409.8 439.8 %reduce-scatter.9.cloned.1.call-start = ((), (), s32[]{:S(2)}) async-start(), calls=%async_computation.12 | async-start | bytes 2048000 | tf_op jit(solution)/shard_map/reduce_scatter | solution.py:377
  421.5 8.0 copy-start.34
  421.5 8.0 copy-start.41
  426.9 2.5 copy-start.25
  429.5 360.7 %copy-start.15 = (bf16[1,384,1024]{2,1,0:T(8,128)(2,1)S(1)}, bf16[1,384,1024]{2,1,0:T(8,128)(2,1)}, u32[]{:S(2)}) copy-start(bf16[1,384,1024]{2,1,0:T(8,128)(2,1)} %param.34) | copy-start | bytes 2359300
  429.5 360.7 %copy-start.45 = (f32[4,1,256]{2,1,0:T(1,128)S(1)}, f32[4,1,256]{2,1,0:T(1,128)}, u32[]{:S(2)}) copy-start(f32[4,1,256]{2,1,0:T(1,128)} %copy-done.44) | copy-start | bytes 12292
  429.5 360.7 %copy-start.52 = (f32[384]{0:T(512)S(1)}, f32[384]{0:T(512)}, u32[]{:S(2)}) copy-start(f32[384]{0:T(512)} %copy-done.51) | copy-start | bytes 4612
  790.2 3.6 copy-start.36
  793.7 113.2 %reduce-scatter.13.cloned.1.call-start = ((), (), s32[]{:S(2)}) async-start(), calls=%async_computation.14 | async-start | bytes 7208960 | tf_op jit(solution)/shard_map/reduce_scatter | solution.py:386
  800.7 163.3 %reduce-scatter.15.cloned.1.call-start = ((), (), s32[]{:S(2)}) async-start(), calls=%async_computation.15 | async-start | bytes 7208960 | tf_op jit(solution)/shard_map/reduce_scatter | solution.py:389
  807.7 213.7 %reduce-scatter.17.cloned.1.call-start = ((), (), s32[]{:S(2)}) async-start(), calls=%async_computation.16 | async-start | bytes 7208960 | tf_op jit(solution)/shard_map/reduce_scatter | solution.py:392
  815.6 394.4 %all-reduce.11.cloned.1.call-start = ((), (), s32[]{:S(2)}) async-start(), calls=%async_computation.17 | async-start | bytes 10518528 | tf_op jit(solution)/shard_map/psum | solution.py:398
  1021.3 1.9 copy-start.9
  1023.2 6.7 copy-start.16
  1023.2 6.7 copy-start.56
  1030.0 3.6 copy-start.53
  1030.0 33.3 %copy-start.17 = (bf16[1,384,1024]{2,1,0:T(8,128)(2,1)S(1)}, bf16[1,384,1024]{2,1,0:T(8,128)(2,1)}, u32[]{:S(2)}) copy-start(bf16[1,384,1024]{2,1,0:T(8,128)(2,1)} %param.34) | copy-start | bytes 2359300
  1210.0 3.2 copy-start.32
  1213.2 1.9 copy-start.31
  1215.2 1.9 copy-start.40
  1215.2 3.0 copy-start.42
  (10 other events, 12.7 us)
Sparse Core Ops, SparseCore 0:
  9.5 22.8 all-gather.7
  34.0 22.7 all-gather.9
  58.4 43.3 all-gather.11
  103.2 43.3 all-gather.13
  148.1 43.3 all-gather.15
  406.7 378.0 reduce-scatter.6
  787.4 31.1 reduce-scatter.10
  821.1 28.4 reduce-scatter.8
  852.1 54.7 reduce-scatter.12
  909.3 54.7 reduce-scatter.14
  966.6 54.7 reduce-scatter.16
  1025.5 184.4 all-reduce.10
where the time goes:
time: 1240 us; the launch traced here: 1230 us
  waiting for transfers between devices  725 us (58%)
  matrix products  203 us (16%)
  local copies, waits for them, and re-layouts  130 us (10%)
  other arithmetic  59.7 us (5%)
  blocking collectives  50.1 us (4%)
  loops' own time  43 us (3%)
  between operations  15.8 us (1%)
    reduce_scatter x1, waiting for transfers between devices, local(): lax.psum_scatter((first_back[1] + second_back[1]).astype(jnp.bfloat16), '...  355 us
    psum x1, waiting for transfers between devices, local(): lax.psum(shard_grads[1].astype(jnp.bfloat16), 'rep').astype(jnp.float32)  144 us
    reduce_scatter x1, waiting for transfers between devices, local(): lax.psum_scatter(gate_weight_grad.astype(jnp.bfloat16), 'grp', scatter_di...  57.3 us
    reduce_scatter x1, waiting for transfers between devices, local(): lax.psum_scatter(down_grad.astype(jnp.bfloat16), 'grp', scatter_dimension...  57.3 us
    reduce_scatter x1, waiting for transfers between devices, local(): lax.psum_scatter(up_weight_grad.astype(jnp.bfloat16), 'grp', scatter_dime...  57.1 us
    reduce_scatter x1, waiting for transfers between devices, local(): lax.psum_scatter(factor_weight_grad.astype(jnp.bfloat16), 'grp', scatter_...  31 us
  transfers between devices with their start and end apart: 12, of which 9 were waited for; matrix products, arithmetic and copies ran while one was open for 15% of the time, Pallas kernels for 0%

commit v1 on v0

v1 whole, which is shorter than its diff:
```python
import functools

import jax
import jax.numpy as jnp
from jax import lax
from jax.experimental import pallas as pl
from jax.experimental.pallas import tpu as pltpu
from jax.sharding import PartitionSpec as P

HEADS = 16
HDIM = 64
QRANK = 6
KRANK = 2
PAIRS = HEADS // 2
CUT_Q = QRANK * HEADS
CUT_QB = CUT_Q + QRANK * HDIM
CUT_K = CUT_QB + KRANK * HEADS
CUT_KB = CUT_K + KRANK * HDIM
CUT_V = CUT_KB + KRANK * HEADS
CUT_VB = CUT_V + KRANK * HDIM

bf16 = jnp.bfloat16
f32 = jnp.float32


def dot(spec, left, right):
    return jnp.einsum(spec, left, right, preferred_element_type=f32)


def rms_scale(values):
    return lax.rsqrt(jnp.mean(values * values, axis=-1, keepdims=True) + 1e-05)


def norm_back(grad_hidden, normed, scale, gain):
    grad_normed = grad_hidden * gain
    gain_grad = jnp.sum(grad_hidden * normed, axis=0)
    grad_values = scale * (
        grad_normed - normed * jnp.mean(grad_normed * normed, axis=-1, keepdims=True)
    )
    return gain_grad, grad_values


def swap(value, axis, mask):
    size = lax.axis_size(axis)
    return lax.ppermute(value, axis, [(j, j ^ mask) for j in range(size)])


def bits_down(size):
    mask, out = size // 2, []
    while mask:
        out.append(mask)
        mask //= 2
    return out


def gather_rel(block, axis="grp"):
    have = {0: block}
    for mask in bits_down(lax.axis_size(axis)):
        for s in sorted(have):
            have[s ^ mask] = swap(have[s], axis, mask)
    return [have[s] for s in range(len(have))]


def scatter_rel(parts, axis="grp"):
    parts = dict(enumerate(parts))
    for mask in reversed(bits_down(lax.axis_size(axis))):
        for s in sorted(parts):
            if not s & mask:
                moved = swap(parts[s | mask].astype(bf16), axis, mask)
                parts[s] = parts[s].astype(f32) + moved.astype(f32)
                del parts[s | mask]
    return parts[0]


def exchange_rel(parts, axis="grp"):
    return [part if s == 0 else swap(part, axis, s) for s, part in enumerate(parts)]


def in_order(blocks, own, axis):
    stacked = jnp.stack(blocks)
    return jnp.concatenate(
        [lax.dynamic_index_in_dim(stacked, own ^ j, 0, False) for j in range(len(blocks))],
        axis=axis,
    )


def rel_rows(matrix, own, count):
    pieces = matrix.reshape(count, matrix.shape[0] // count, matrix.shape[1])
    return [lax.dynamic_index_in_dim(pieces, own ^ s, 0, False) for s in range(count)]


def small_sum(value, axis="rep"):
    own = lax.axis_index(axis)
    masks = bits_down(lax.axis_size(axis))[::-1]
    for mask in masks:
        half = value.shape[0] // 2
        upper = (own // mask) % 2 == 1
        keep = jnp.where(upper, value[half:], value[:half])
        send = jnp.where(upper, value[:half], value[half:])
        value = (keep.astype(f32) + swap(send, axis, mask).astype(f32)).astype(bf16)
    for mask in masks[::-1]:
        upper = (own // mask) % 2 == 1
        other = swap(value, axis, mask)
        value = jnp.where(
            upper,
            jnp.concatenate([other, value], axis=0),
            jnp.concatenate([value, other], axis=0),
        )
    return value


def turn(block, cosine, sine):
    rows, tokens = block.shape
    pieces = block.reshape(rows // HDIM, 2, HDIM // 2, tokens)
    first, second = pieces[:, 0], pieces[:, 1]
    return jnp.stack(
        [first * cosine - second * sine, second * cosine + first * sine], axis=1
    ).reshape(rows, tokens)


def turn_factors(values, cosine, sine):
    return jnp.concatenate(
        [
            values[:CUT_Q],
            turn(values[CUT_Q:CUT_QB], cosine, sine),
            values[CUT_QB:CUT_K],
            turn(values[CUT_K:CUT_KB], cosine, sine),
            values[CUT_KB:],
        ],
        axis=0,
    )


def by_pair(heads_part, ranks):
    tokens = heads_part.shape[1]
    return (
        heads_part.reshape(ranks, PAIRS, 2, tokens)
        .transpose(1, 2, 0, 3)
        .reshape(PAIRS, 2 * ranks, tokens)
    )


def from_pair(parts, ranks):
    tokens = parts.shape[2]
    return (
        parts.reshape(PAIRS, 2, ranks, tokens)
        .transpose(2, 0, 1, 3)
        .reshape(ranks * HEADS, tokens)
    )


def expand(a_ref, b_ref, head, ranks):
    total = None
    for r in range(ranks):
        term = b_ref[r * HDIM : (r + 1) * HDIM, :] * a_ref[0, head * ranks + r, :][None, :]
        total = term if total is None else total + term
    return (total / ranks).astype(bf16)


def fill_bias(limit_ref, row_ref, square_ref):
    @pl.when(pl.program_id(0) == 0)
    def _():
        column = lax.broadcasted_iota(jnp.int32, row_ref.shape, 1)
        row_ref[...] = jnp.where(column < limit_ref[0], 0.0, -1e30)
        rows = lax.broadcasted_iota(jnp.int32, square_ref.shape, 0)
        columns = lax.broadcasted_iota(jnp.int32, square_ref.shape, 1)
        square_ref[...] = jnp.where(columns <= rows, 0.0, -1e30)


def rows_by_rows(left, right):
    return lax.dot_general(left, right, (((1,), (1,)), ((), ())), preferred_element_type=f32)


def plain(left, right):
    return jnp.dot(left, right, preferred_element_type=f32)


def forward_kernel(
    prefix, limit_ref, aq, bq, ak, bk, av, bv, out_ref, log_ref, row_ref, square_ref
):
    fill_bias(limit_ref, row_ref, square_ref)
    outs, logs = [], []
    for head in range(2):
        q = (expand(aq, bq, head, QRANK).astype(f32) * HDIM**-0.5).T.astype(bf16)
        k = expand(ak, bk, head, KRANK)
        v = expand(av, bv, head, KRANK)
        s_far = plain(q, k[:, :prefix]) + row_ref[0:1, :]
        s_own = plain(q, k[:, prefix:]) + square_ref[...]
        top = jnp.maximum(
            jnp.max(s_far, axis=1, keepdims=True), jnp.max(s_own, axis=1, keepdims=True)
        )
        e_far, e_own = jnp.exp(s_far - top), jnp.exp(s_own - top)
        mass = jnp.sum(e_far, axis=1, keepdims=True) + jnp.sum(e_own, axis=1, keepdims=True)
        share = 1.0 / mass
        outs.append(
            rows_by_rows((e_far * share).astype(bf16), v[:, :prefix])
            + rows_by_rows((e_own * share).astype(bf16), v[:, prefix:])
        )
        logs.append(jnp.broadcast_to(top + jnp.log(mass), (q.shape[0], HDIM)))
    out_ref[...] = jnp.concatenate(outs, axis=1).astype(bf16)
    log_ref[0] = jnp.concatenate(logs, axis=1)


def backward_kernel(
    prefix, limit_ref, aq, bq, ak, bk, av, bv, do_ref, o_ref, log_ref,
    daq, dbq, dak, dbk, dav, dbv, row_ref, square_ref,
):
    fill_bias(limit_ref, row_ref, square_ref)

    @pl.when(pl.program_id(0) == 0)
    def _():
        dbq[...] = jnp.zeros_like(dbq)
        dbk[...] = jnp.zeros_like(dbk)
        dbv[...] = jnp.zeros_like(dbv)

    def factor_grads(grad, head, ranks, a_ref, b_ref, da_ref, db_ref):
        grad = grad / ranks
        for r in range(ranks):
            rows = slice(r * HDIM, (r + 1) * HDIM)
            spot = head * ranks + r
            da_ref[0, spot : spot + 1, :] = jnp.sum(grad * b_ref[rows, :], axis=0, keepdims=True)
            db_ref[rows, :] += grad * a_ref[0, spot, :][None, :]

    do_all = do_ref[...]
    do_turned = do_all.astype(f32).T.astype(bf16)
    products = do_all.astype(f32) * o_ref[...].astype(f32)
    for head in range(2):
        cols = slice(head * HDIM, (head + 1) * HDIM)
        q_turned = expand(aq, bq, head, QRANK).astype(f32) * HDIM**-0.5
        q = q_turned.T.astype(bf16)
        q_turned = q_turned.astype(bf16)
        k = expand(ak, bk, head, KRANK)
        v = expand(av, bv, head, KRANK)
        log_total = log_ref[0][:, head * HDIM : head * HDIM + 1]
        delta = jnp.sum(products[:, cols], axis=1, keepdims=True)
        do_head = do_all[:, cols]
        grad_q = None
        grads_k, grads_v = [], []
        for low, high, bias in (
            (0, prefix, row_ref[0:1, :]),
            (prefix, k.shape[1], square_ref[...]),
        ):
            k_part, v_part = k[:, low:high], v[:, low:high]
            probs = jnp.exp(plain(q, k_part) + bias - log_total)
            grad_s = (probs * (plain(do_head, v_part) - delta)).astype(bf16)
            part = rows_by_rows(grad_s, k_part)
            grad_q = part if grad_q is None else grad_q + part
            grads_k.append(plain(q_turned, grad_s))
            grads_v.append(plain(do_turned[cols], probs.astype(bf16)))
        factor_grads((grad_q * HDIM**-0.5).T, head, QRANK, aq, bq, daq, dbq)
        factor_grads(jnp.concatenate(grads_k, axis=1), head, KRANK, ak, bk, dak, dbk)
        factor_grads(jnp.concatenate(grads_v, axis=1), head, KRANK, av, bv, dav, dbv)


def pair_spec(rows, tokens):
    return pl.BlockSpec((1, rows, tokens), lambda p: (p, 0, 0))


def whole_spec(rows, tokens):
    return pl.BlockSpec((rows, tokens), lambda p: (0, 0))


def attention_specs(tokens, keys):
    return [
        pl.BlockSpec(memory_space=pltpu.SMEM),
        pair_spec(2 * QRANK, tokens),
        whole_spec(QRANK * HDIM, tokens),
        pair_spec(2 * KRANK, keys),
        whole_spec(KRANK * HDIM, keys),
        pair_spec(2 * KRANK, keys),
        whole_spec(KRANK * HDIM, keys),
    ]


def attention_forward(limit, factors, tokens, keys):
    prefix = keys - tokens
    column = pl.BlockSpec((tokens, 2 * HDIM), lambda p: (0, p))
    return pl.pallas_call(
        functools.partial(forward_kernel, prefix),
        grid=(PAIRS,),
        in_specs=attention_specs(tokens, keys),
        out_specs=[column, pair_spec(tokens, 2 * HDIM)],
        out_shape=[
            jax.ShapeDtypeStruct((tokens, HEADS * HDIM), bf16),
            jax.ShapeDtypeStruct((PAIRS, tokens, 2 * HDIM), f32),
        ],
        scratch_shapes=[pltpu.VMEM((8, prefix), f32), pltpu.VMEM((tokens, tokens), f32)],
        cost_estimate=pl.CostEstimate(
            flops=16 * HEADS * tokens * keys * HDIM,
            bytes_accessed=8 * tokens * HEADS * HDIM,
            transcendentals=HEADS * tokens * keys,
        ),
        name="attend",
    )(limit, *factors)


def attention_backward(limit, factors, do, o, logs, tokens, keys):
    prefix = keys - tokens
    column = pl.BlockSpec((tokens, 2 * HDIM), lambda p: (0, p))
    shapes = [
        (PAIRS, 2 * QRANK, tokens),
        (QRANK * HDIM, tokens),
        (PAIRS, 2 * KRANK, keys),
        (KRANK * HDIM, keys),
        (PAIRS, 2 * KRANK, keys),
        (KRANK * HDIM, keys),
    ]
    return pl.pallas_call(
        functools.partial(backward_kernel, prefix),
        grid=(PAIRS,),
        in_specs=attention_specs(tokens, keys)
        + [column, column, pair_spec(tokens, 2 * HDIM)],
        out_specs=attention_specs(tokens, keys)[1:],
        out_shape=[jax.ShapeDtypeStruct(shape, f32) for shape in shapes],
        scratch_shapes=[pltpu.VMEM((8, prefix), f32), pltpu.VMEM((tokens, tokens), f32)],
        cost_estimate=pl.CostEstimate(
            flops=40 * HEADS * tokens * keys * HDIM,
            bytes_accessed=16 * tokens * HEADS * HDIM,
            transcendentals=HEADS * tokens * keys,
        ),
        name="attend_back",
    )(limit, *factors, do, o, logs)


def local(
    layer_input,
    branch,
    attention_gain,
    factor_weight,
    output_weight,
    feed_gain,
    gate_weight,
    up_weight,
    down_weight,
    cotangent,
):
    count = lax.axis_size("grp")
    own = lax.axis_index("grp")
    half = count // 2
    tokens, width = layer_input.shape[1:]
    rows = factor_weight.shape[0]
    fac = factor_weight.shape[1]
    feed = down_weight.shape[0]
    prefix = tokens * half
    keys = prefix + tokens
    upstream = cotangent[0]

    packed = jnp.concatenate(
        [factor_weight, attention_gain[:, None], feed_gain[:, None]], axis=1
    )
    packed = in_order(gather_rel(packed), own, 0)
    factor_full = packed[:, :fac]
    gain_one = packed[:, fac].astype(f32)
    gain_two = packed[:, fac + 1].astype(f32)

    lane = own - half
    chosen = jnp.sum(jnp.where(jnp.arange(branch.shape[1]) == lane, branch[0], 0))
    is_prompt = own < half
    start = jnp.where(is_prompt, own * tokens, chosen)
    positions = start + jnp.arange(tokens, dtype=jnp.int32)
    limit = start.astype(jnp.int32).reshape(1)
    freqs = 10000.0 ** (-jnp.arange(HDIM // 2).astype(f32) / (HDIM // 2))
    phase = freqs[:, None] * positions.astype(f32)[None, :]
    cosine, sine = jnp.cos(phase), jnp.sin(phase)

    residual_in = layer_input[0].astype(f32)
    scale_one = rms_scale(residual_in)
    normed_one = residual_in * scale_one
    hidden_one = (normed_one * gain_one).astype(bf16)
    raw = dot("df,td->ft", factor_full, hidden_one)
    factors = turn_factors(raw, cosine, sine).astype(bf16)

    table = factors[CUT_QB:]
    arrived = lax.ppermute(table, "grp", [(j, j + half) for j in range(half)])
    have = {0: jnp.where(is_prompt, table, arrived)}
    for mask in bits_down(half):
        for s in sorted(have):
            have[s ^ mask] = swap(have[s], "grp", mask)
    low_own = own % half
    table_all = jnp.concatenate(
        [in_order([have[s] for s in range(half)], low_own, 1), table], axis=1
    ).astype(f32)
    o_k, o_kb, o_v = CUT_K - CUT_QB, CUT_KB - CUT_QB, CUT_V - CUT_QB
    attention_in = (
        by_pair(factors[:CUT_Q].astype(f32), QRANK),
        factors[CUT_Q:CUT_QB].astype(f32),
        by_pair(table_all[:o_k], KRANK),
        table_all[o_k:o_kb],
        by_pair(table_all[o_kb:o_v], KRANK),
        table_all[o_v:],
    )
    attended, logs = attention_forward(limit, attention_in, tokens, keys)

    def own_columns(weight):
        pieces = weight.reshape(rows, count, feed).transpose(1, 0, 2)
        parts = [lax.dynamic_index_in_dim(pieces, own ^ s, 0, False) for s in range(count)]
        return in_order(exchange_rel(parts), own, 0)

    output_full = in_order(gather_rel(output_weight), own, 0)
    gate_full = own_columns(gate_weight)
    up_full = own_columns(up_weight)
    upstream_all = jnp.concatenate(gather_rel(upstream), axis=0)

    middle = residual_in + dot("tf,fd->td", attended, output_full)
    scale_two = rms_scale(middle)
    normed_two = middle * scale_two
    hidden_two = (normed_two * gain_two).astype(bf16)
    hidden_all = jnp.concatenate(gather_rel(hidden_two), axis=0)

    active_grad = dot("td,fd->tf", upstream_all, down_weight)
    gate = dot("td,df->tf", hidden_all, gate_full)
    up = dot("td,df->tf", hidden_all, up_full)
    sig = jax.nn.sigmoid(gate)
    active = (gate * sig * up).astype(bf16)
    gate_grad = (active_grad * up * sig * (1.0 + gate * (1.0 - sig))).astype(bf16)
    up_grad = (active_grad * gate * sig).astype(bf16)

    def blocks(matrix):
        return [matrix[s * tokens : (s + 1) * tokens] for s in range(count)]

    hidden_grad = dot("tf,df->td", gate_grad, gate_full) + dot("tf,df->td", up_grad, up_full)
    hidden_two_grad = scatter_rel(blocks(hidden_grad))
    result = middle + scatter_rel(blocks(dot("tf,fd->td", active, down_weight)))

    down_grad = dot("tf,td->fd", active, upstream_all).astype(bf16)
    gate_weight_grad = dot("td,tf->df", hidden_all, gate_grad).astype(bf16)
    up_weight_grad = dot("td,tf->df", hidden_all, up_grad).astype(bf16)

    def own_rows(grad):
        return jnp.stack(exchange_rel(rel_rows(grad, own, count)))

    gate_pieces = own_rows(gate_weight_grad)
    up_pieces = own_rows(up_weight_grad)

    feed_gain_grad, middle_grad = norm_back(hidden_two_grad, normed_two, scale_two, gain_two)
    middle_grad = middle_grad + upstream.astype(f32)
    branch_grad = middle_grad.astype(bf16)
    output_weight_grad = dot("tf,td->fd", attended, branch_grad)
    output_piece = scatter_rel(rel_rows(output_weight_grad, own, count)).astype(bf16)
    grad_heads = dot("td,fd->tf", branch_grad, output_full).astype(bf16)

    gate_sum, up_sum, down_sum, output_sum = lax.psum(
        (gate_pieces, up_pieces, down_grad, output_piece), "rep"
    )

    def final_columns(pieces):
        return in_order([pieces[s] for s in range(count)], own, 1).astype(f32)

    daq, dbq, dak, dbk, dav, dbv = attention_backward(
        limit, attention_in, grad_heads, attended, logs, tokens, keys
    )
    table_grad = jnp.concatenate(
        [from_pair(dak, KRANK), dbk, from_pair(dav, KRANK), dbv], axis=0
    )
    far = table_grad[:, :prefix].reshape(-1, half, tokens)
    far = far.transpose(1, 0, 2)
    parts = {s: lax.dynamic_index_in_dim(far, low_own ^ s, 0, False) for s in range(half)}
    for mask in reversed(bits_down(half)):
        for s in sorted(parts):
            if not s & mask:
                parts[s] = parts[s] + swap(parts[s | mask].astype(bf16), "grp", mask).astype(f32)
                del parts[s | mask]
    back = lax.ppermute(parts[0].astype(bf16), "grp", [(j + half, j) for j in range(half)])
    own_table = table_grad[:, prefix:] + jnp.where(is_prompt, parts[0] + back.astype(f32), 0.0)

    factor_grad = jnp.concatenate([from_pair(daq, QRANK), dbq, own_table], axis=0)
    raw_grad = turn_factors(factor_grad, cosine, -sine).astype(bf16)
    factor_weight_grad = dot("td,ft->df", hidden_one, raw_grad)
    hidden_one_grad = dot("ft,df->td", raw_grad, factor_full)
    attention_gain_grad, input_part = norm_back(hidden_one_grad, normed_one, scale_one, gain_one)
    input_grad = middle_grad + input_part

    tail = jnp.concatenate(
        [factor_weight_grad, attention_gain_grad[:, None], feed_gain_grad[:, None]], axis=1
    )
    tail = scatter_rel(rel_rows(tail, own, count)).astype(bf16)
    tail = small_sum(tail).astype(f32)

    return (
        result.astype(bf16)[None],
        input_grad[None],
        tail[:, fac],
        tail[:, :fac],
        output_sum.astype(f32),
        tail[:, fac + 1],
        final_columns(gate_sum),
        final_columns(up_sum),
        down_sum.astype(f32),
    )


def solution(mesh):
    specs = (
        P("rep", "grp", None),
        P("rep", None),
        P("grp"),
        P("grp", None),
        P("grp", None),
        P("grp"),
        P("grp", None),
        P("grp", None),
        P("grp", None),
        P("rep", "grp", None),
    )
    out_specs = (
        P("rep", "grp", None),
        P("rep", "grp", None),
        P("grp"),
        P("grp", None),
        P("grp", None),
        P("grp"),
        P("grp", None),
        P("grp", None),
        P("grp", None),
    )
    return jax.shard_map(local, mesh=mesh, in_specs=specs, out_specs=out_specs, check_vma=False)
```

time: 1240 us -> 558 us (0.45)
  waiting for transfers between devices: 725 us -> 294 us
  matrix products: 203 us -> 55.7 us
  local copies, waits for them, and re-layouts: 130 us -> 62.8 us
  blocking collectives: 50.1 us -> 0 us
  Pallas kernels: 0 us -> 47.6 us
  loops' own time: 43 us -> 0 us
  starting transfers between devices: 0.48 us -> 36.3 us
  other arithmetic: 59.7 us -> 40.4 us
    reduce_scatter x6 -> x0, waiting for transfers between devices: 560 us -> none  [the longest x1 355 us: local(): lax.psum_scatter((first_back[1] + second_back[1]).astype(jnp.bfloat16), '...]
    ppermute x0 -> x46, waiting for transfers between devices: none -> 216 us  [the longest x44 204 us: swap(): return lax.ppermute(value, axis, [(j, j ^ mask) for j in range(size)])]
    dot_general x54 -> x15, matrix products: 203 us -> 55.7 us  [dot(): return jnp.einsum(spec, left, right, preferred_element_type=f32)]
    psum x1, waiting for transfers between devices: 144 us -> 77.7 us  [local(): lax.psum((gate_pieces, up_pieces, down_grad, output_piece), 'rep')]
    pallas_call x0 -> x2, Pallas kernels: none -> 47.6 us  [the longest x1 26.6 us: attention_backward(): pl.pallas_call(functools.partial(backward_kernel, prefix), grid=(PAIRS,),...]
    another operation x24 -> x0, loops' own time: 43 us -> none  [the longest x2 21.3 us: half_backward(): lax.scan(grad_step, jnp.zeros((local_rows, head_span, HDIM), jnp.float32)...]
    ppermute x0 -> x46, starting transfers between devices: none -> 36.3 us  [the longest x44 31.3 us: swap(): return lax.ppermute(value, axis, [(j, j ^ mask) for j in range(size)])]
    reduce_or x18 -> x0, other arithmetic: 25.9 us -> none  [the longest x6 10 us: grad_step(): return lax.cond(jnp.any(visible_now), grad_update, skip_block, carry)]
  transfers between devices with their start and end apart: 12 -> 47, of which waited for: 9 -> 23; matrix products, arithmetic and copies ran while one was open for 15% -> 13% of each run, Pallas kernels for 0% -> 0%
where the time goes in v1:
time: 558 us; the launch traced here: 553 us
  waiting for transfers between devices  294 us (53%)
  local copies, waits for them, and re-layouts  62.8 us (11%)
  matrix products  55.7 us (10%)
  Pallas kernels  47.6 us (9%)
  other arithmetic  40.4 us (7%)
  starting transfers between devices  36.3 us (7%)
  between operations  16.2 us (3%)
    ppermute x44, waiting for transfers between devices, swap(): return lax.ppermute(value, axis, [(j, j ^ mask) for j in range(size)])  204 us
    psum x1, waiting for transfers between devices, local(): lax.psum((gate_pieces, up_pieces, down_grad, output_piece), 'rep')  77.7 us
    dot_general x15, matrix products, dot(): return jnp.einsum(spec, left, right, preferred_element_type=f32)  55.7 us
    ppermute x44, starting transfers between devices, swap(): return lax.ppermute(value, axis, [(j, j ^ mask) for j in range(size)])  31.3 us
    pallas_call x1, Pallas kernels, attention_backward(): pl.pallas_call(functools.partial(backward_kernel, prefix), grid=(PAIRS,),...  26.6 us
    pallas_call x1, Pallas kernels, attention_forward(): pl.pallas_call(functools.partial(forward_kernel, prefix), grid=(PAIRS,),...  21 us
    unnamed x112, local copies, waits for them, and re-layouts  18.1 us
  transfers between devices with their start and end apart: 47, of which 23 were waited for; matrix products, arithmetic and copies ran while one was open for 13% of the time, Pallas kernels for 0%

profile of v1, /device:TPU:0, one launch (start us, length us, event | category | flops | bytes accessed | tf_op | source)
XLA Modules:
  0.0 552.7 jit_solution(9356986128955798861)
XLA Ops:
  7.2 3.0 collective-permute-start.6
  11.6 1.8 fusion.61
  17.3 14.0 %collective-permute-done.1 = bf16[256,802]{0,1:T(8,128)(2,1)S(1)} collective-permute-done((bf16[256,802]{0,1:T(8,128)(2,1)}, bf16[256,802]{0,1:T(8,128)(2,1)S(1)}, u32[]{:S(2)}, u32[]{:S(2)}) %collective-permute-start.1) | collective-permute-done | bytes 410656 | tf_op jit(solution)/shard_map/ppermute | solution.py:45
  36.8 3.7 collective-permute-start.3
  41.4 4.5 collective-permute-done.3
  54.7 21.0 %attend.1 = (bf16[384,1024]{1,0:T(8,128)(2,1)}, f32[8,384,128]{2,1,0:T(8,128)}) custom-call(s32[1]{0:T(128)} %bitcast.2.limit_ref, f32[8,12,384]{2,1,0:T(8,128)} %copy.59.aq, f32[384,384]{1,0:T(8,128)} %bitcast_convert_fusion.bq, f32[8,4,1152]{2,1,0:T(4,128)} %reshape.281.ak, f32[128,1152]{1,0:T(8,128)} %slice.207.bk, f32[8,4,1152]{2,1,0:T(4,128)} %reshape.283.av, ...), custom_call_target="tpu_custom_call" | custom-call | flops 7247757312 | bytes 3145728 | tf_op jit(solution)/shard_map/attend/pallas_call | solution.py:278
  75.7 3.1 multiply_reduce_fusion.2
  80.1 2.5 collective-permute-start.9
  82.6 2.5 copy.60
  85.1 2.3 dynamic-slice_bitcast_fusion.31
  87.5 1.7 collective-permute-start.12
  89.3 2.5 copy.61
  93.7 14.9 %collective-permute-done.13 = bf16[256,704]{0,1:T(8,128)(2,1)} collective-permute-done((bf16[256,704]{0,1:T(8,128)(2,1)}, bf16[256,704]{0,1:T(8,128)(2,1)}, u32[]{:S(2)}, u32[]{:S(2)}) %collective-permute-start.13) | collective-permute-done | bytes 360480 | tf_op jit(solution)/shard_map/ppermute | solution.py:45
  110.0 6.7 %collective-permute-done.12 = bf16[256,704]{0,1:T(8,128)(2,1)} collective-permute-done((bf16[256,704]{0,1:T(8,128)(2,1)}, bf16[256,704]{0,1:T(8,128)(2,1)}, u32[]{:S(2)}, u32[]{:S(2)}) %collective-permute-start.12) | collective-permute-done | bytes 360480 | tf_op jit(solution)/shard_map/ppermute | solution.py:45
  117.2 2.0 collective-permute-start.15
  119.3 4.7 collective-permute-done.16
  125.7 23.0 %collective-permute-done.15 = bf16[256,704]{0,1:T(8,128)(2,1)S(1)} collective-permute-done((bf16[256,704]{0,1:T(8,128)(2,1)S(1)}, bf16[256,704]{0,1:T(8,128)(2,1)S(1)}, u32[]{:S(2)}, u32[]{:S(2)}) %collective-permute-start.15) | collective-permute-done | bytes 360480 | tf_op jit(solution)/shard_map/ppermute | solution.py:45
  149.7 4.4 fusion.41
  154.1 3.8 fusion.43
  157.9 10.0 %multiply_convert_fusion = (bf16[1536,704]{0,1:T(8,128)(2,1)}, bf16[1536,704]{0,1:T(8,128)(2,1)S(1)}, bf16[1536,704]{0,1:T(8,128)(2,1)}) fusion(f32[1536,704]{0,1:T(8,128)S(1)} %fusion.43, f32[1536,704]{0,1:T(8,128)S(1)} %fusion.41, bf16[704,1024]{1,0:T(8,128)(2,1)S(1)} %copy-done, bf16[384,1024]{1,0:T(8,128)(2,1)S(1)} %collective-permute-done.22, ...), kind=kOutput, calls=%fused_computation | convolution fusion | flops 2244476928 | bytes 19726336 | tf_op jit(solution)/shard_map/td,fd->tf/dot_general | solution.py:27
  167.9 5.2 fusion.42
  173.2 4.9 convolution_convert_fusion.1
  178.1 4.0 reshape.298
  182.1 6.0 %convolution_convert_fusion = bf16[1024,704]{0,1:T(8,128)(2,1)} fusion(bf16[1536,704]{0,1:T(8,128)(2,1)} %get-tuple-element.44, bf16[384,1024]{1,0:T(8,128)(2,1)} %copy-done.42, bf16[384,1024]{1,0:T(8,128)(2,1)} %collective-permute-done.9, bf16[384,1024]{1,0:T(8,128)(2,1)} %copy-done.41, bf16[384,1024]{1,0:T(8,128)(2,1)} %multiply_convert_fusion.3), kind=kOutput, calls=%fused_computation.19 | convolution fusion | flops 2227896320 | bytes 6750208 | tf_op jit(solution)/shard_map/td,tf->df/dot_general | solution.py:27
  188.1 4.0 reshape.299
  192.1 6.4 %constant_dynamic-slice_fusion.3 = (bf16[1,256,704]{1,0,2:T(2,128)(2,1)S(1)}, bf16[1,256,704]{1,0,2:T(2,128)(2,1)S(1)}, bf16[1,256,704]{1,0,2:T(2,128)(2,1)S(1)}, bf16[1,256,704]{1,0,2:T(2,128)(2,1)S(1)}) fusion(bf16[4,256,704]{1,0,2:T(4,128)(2,1)} %reshape.299, s32[]{:T(128)S(6)} %select_n.186, s32[]{:T(128)S(6)} %select_n.188, s32[]{:T(128)S(6)} %select_n.187, ...), kind=kLoop, calls=%fused_computation.186 | loop fusion | bytes 2883600 | tf_op jit(solution)/shard_map/jit(dynamic_index_in_dim)/dynamic_slice | solution.py:89
  198.7 1.9 collective-permute-start.45
  201.2 3.0 constant_dynamic-slice_fusion.7
  205.7 2.7 fusion.67
  210.0 2.7 fusion.68
  214.4 3.6 collective-permute-done.44
  217.9 1.7 collective-permute-start.25
  219.7 3.5 convolution_convert_fusion.2
  225.5 1.7 collective-permute-start.19
  228.5 21.7 %collective-permute-done.41 = bf16[256,704]{0,1:T(8,128)(2,1)S(1)} collective-permute-done((bf16[256,704]{0,1:T(8,128)(2,1)S(1)}, bf16[256,704]{0,1:T(8,128)(2,1)S(1)}, u32[]{:S(2)}, u32[]{:S(2)}) %collective-permute-start.41) | collective-permute-done | bytes 360480 | tf_op jit(solution)/shard_map/ppermute | solution.py:45
  252.2 14.3 %collective-permute-done.19 = bf16[384,1024]{1,0:T(8,128)(2,1)S(1)} collective-permute-done((bf16[384,1024]{1,0:T(8,128)(2,1)S(1)}, bf16[384,1024]{1,0:T(8,128)(2,1)S(1)}, u32[]{:S(2)}, u32[]{:S(2)}) %collective-permute-start.19) | collective-permute-done | bytes 786464 | tf_op jit(solution)/shard_map/ppermute | solution.py:45
  266.5 3.2 convert_add_fusion.1
  269.8 1.9 convolution_convert_fusion.3.do_ref
  271.7 3.3 fusion.37
  275.0 26.6 %attend_back.1 = (f32[8,12,384]{2,1,0:T(8,128)}, f32[384,384]{1,0:T(8,128)}, f32[8,4,1152]{2,1,0:T(4,128)}, f32[128,1152]{1,0:T(8,128)}, f32[8,4,1152]{2,1,0:T(4,128)}, /*index=5*/f32[128,1152]{1,0:T(8,128)}) custom-call(s32[1]{0:T(128)} %bitcast.2.limit_ref, f32[8,12,384]{2,1,0:T(8,128)} %copy.59.aq, f32[384,384]{1,0:T(8,128)} %bitcast_convert_fusion.bq, ...), custom_call_target="tpu_custom_call" | custom-call | flops 18119393280 | bytes 6291456 | tf_op jit(solution)/shard_map/attend_back/pallas_call | solution.py:308
  306.5 1.7 reshape.294
  308.8 2.7 fusion.32
  312.3 1.6 constant_dynamic-slice_fusion.9
  316.5 7.6 %collective-permute-done.27 = bf16[320,384]{1,0:T(8,128)(2,1)S(1)} collective-permute-done((bf16[320,384]{1,0:T(8,128)(2,1)S(1)}, bf16[320,384]{1,0:T(8,128)(2,1)S(1)}, u32[]{:S(2)}, u32[]{:S(2)}) %collective-permute-start.27) | collective-permute-done | bytes 245792 | tf_op jit(solution)/shard_map/ppermute | solution.py:463
  325.5 1.7 fusion.22
  331.0 2.3 copy.79
  333.2 7.5 %collective-permute-done.39 = bf16[256,1024]{1,0:T(8,128)(2,1)S(1)} collective-permute-done((bf16[256,1024]{1,0:T(8,128)(2,1)S(1)}, bf16[256,1024]{1,0:T(8,128)(2,1)S(1)}, u32[]{:S(2)}, u32[]{:S(2)}) %collective-permute-start.39) | collective-permute-done | bytes 524320 | tf_op jit(solution)/shard_map/ppermute | solution.py:45
  340.7 2.4 fusion.24
  344.2 2.2 fusion.29
  349.3 11.2 %collective-permute-done.30 = bf16[256,802]{0,1:T(8,128)(2,1)} collective-permute-done((bf16[256,802]{0,1:T(8,128)(2,1)S(1)}, bf16[256,802]{0,1:T(8,128)(2,1)}, u32[]{:S(2)}, u32[]{:S(2)}) %collective-permute-start.30) | collective-permute-done | bytes 410656 | tf_op jit(solution)/shard_map/ppermute | solution.py:45
  363.7 9.2 %collective-permute-done.31 = bf16[128,802]{0,1:T(8,128)(2,1)S(1)} collective-permute-done((bf16[128,802]{0,1:T(8,128)(2,1)S(1)}, bf16[128,802]{0,1:T(8,128)(2,1)S(1)}, u32[]{:S(2)}, u32[]{:S(2)}) %collective-permute-start.31) | collective-permute-done | bytes 205344 | tf_op jit(solution)/shard_map/ppermute | solution.py:45
  374.7 22.7 %collective-permute-done.32 = bf16[64,802]{0,1:T(8,128)(2,1)S(1)} collective-permute-done((bf16[64,802]{0,1:T(8,128)(2,1)S(1)}, bf16[64,802]{0,1:T(8,128)(2,1)S(1)}, u32[]{:S(2)}, u32[]{:S(2)}) %collective-permute-start.32) | collective-permute-done | bytes 102688 | tf_op jit(solution)/shard_map/ppermute | solution.py:45
  397.7 16.6 %collective-permute-done.33 = bf16[32,802]{0,1:T(8,128)(2,1)S(1)} collective-permute-done((bf16[32,802]{0,1:T(8,128)(2,1)S(1)}, bf16[32,802]{0,1:T(8,128)(2,1)S(1)}, u32[]{:S(2)}, u32[]{:S(2)}) %collective-permute-start.33) | collective-permute-done | bytes 51360 | tf_op jit(solution)/shard_map/ppermute | solution.py:45
  414.6 17.2 %collective-permute-done.34 = bf16[32,802]{0,1:T(8,128)(2,1)S(1)} collective-permute-done((bf16[32,802]{0,1:T(8,128)(2,1)S(1)}, bf16[32,802]{0,1:T(8,128)(2,1)S(1)}, u32[]{:S(2)}, u32[]{:S(2)}) %collective-permute-start.34) | collective-permute-done | bytes 51360 | tf_op jit(solution)/shard_map/ppermute | solution.py:45
  433.2 9.7 %collective-permute-done.35 = bf16[64,802]{0,1:T(8,128)(2,1)S(1)} collective-permute-done((bf16[64,802]{0,1:T(8,128)(2,1)S(1)}, bf16[64,802]{0,1:T(8,128)(2,1)S(1)}, u32[]{:S(2)}, u32[]{:S(2)}) %collective-permute-start.35) | collective-permute-done | bytes 102688 | tf_op jit(solution)/shard_map/ppermute | solution.py:45
  443.1 1.7 collective-permute-start.36
  446.4 3.7 collective-permute-done.36
  451.8 77.7 %all-reduce.3.cloned.1.call-done = (bf16[256,1024]{1,0:T(8,128)(2,1)}, bf16[4,256,704]{1,2,0:T(8,128)(2,1)}, bf16[4,256,704]{1,2,0:T(8,128)(2,1)}, bf16[704,1024]{1,0:T(8,128)(2,1)}) async-done(((bf16[256,1024]{1,0:T(8,128)(2,1)}, bf16[4,256,704]{1,2,0:T(8,128)(2,1)}, bf16[4,256,704]{1,2,0:T(8,128)(2,1)}, bf16[704,1024]{1,0:T(8,128)(2,1)}), (bf16[256,1024]{1,0:T(8,128)(2,1)}, ...) | async-done | bytes 4849680 | tf_op jit(solution)/shard_map/psum | solution.py:442
  529.5 2.2 convert_element_type.284
  533.2 1.8 maximum_convert_fusion.1
  535.0 3.4 copy.78
  538.4 1.8 maximum_convert_fusion
  540.2 3.5 copy.77
  543.7 1.9 convert_element_type.290
  (273 shorter events, 68.0 us)
Async XLA Ops:
  7.2 150.8 %copy-start = (bf16[704,1024]{1,0:T(8,128)(2,1)S(1)}, bf16[704,1024]{1,0:T(8,128)(2,1)}, u32[]{:S(2)}) copy-start(bf16[704,1024]{1,0:T(8,128)(2,1)} %param.18) | copy-start | bytes 4325380
  7.2 522.3 %all-reduce.3.cloned.1.call-start = ((), (), s32[]{:S(2)}) async-start(), calls=%async_computation | async-start | bytes 9699328 | tf_op jit(solution)/shard_map/psum | solution.py:442
  7.2 24.3 %collective-permute-start.6 = (bf16[256,1024]{1,0:T(8,128)(2,1)}, bf16[256,1024]{1,0:T(8,128)(2,1)}, u32[]{:S(2)}, u32[]{:S(2)}) collective-permute-start(bf16[256,1024]{1,0:T(8,128)(2,1)} %param.14), channel_id=1, source_target_pairs={{0,2},{1,3},{2,0},{3,1},{4,6},{5,7},{6,4},{7,5},{8,10},{9,11},{10,... | collective-permute-start | bytes 1572872 | tf_op jit(solution)/shard_map/ppermute | solution.py:45
  10.3 35.8 %collective-permute-start.5 = (bf16[256,1024]{1,0:T(8,128)(2,1)}, bf16[256,1024]{1,0:T(8,128)(2,1)}, u32[]{:S(2)}, u32[]{:S(2)}) collective-permute-start(bf16[256,1024]{1,0:T(8,128)(2,1)} %param.14), channel_id=1, source_target_pairs={{0,1},{1,0},{2,3},{3,2},{4,5},{5,4},{6,7},{7,6},{8,9},{9,8},{10,11... | collective-permute-start | bytes 1572872 | tf_op jit(solution)/shard_map/ppermute | solution.py:45
  13.4 18.7 %collective-permute-start = (bf16[256,802]{0,1:T(8,128)(2,1)}, bf16[256,802]{0,1:T(8,128)(2,1)S(1)}, u32[]{:S(2)}, u32[]{:S(2)}) collective-permute-start(bf16[256,802]{0,1:T(8,128)(2,1)} %get-tuple-element.111), channel_id=1, source_target_pairs={{0,1},{1,0},{2,3},{3,2},{4,5},{5,4},{6,7},{7,6},{8,9},{9,8},{10,11... | collective-permute-start | bytes 1231880 | tf_op jit(solution)/shard_map/ppermute | solution.py:45
  13.9 17.4 %collective-permute-start.1 = (bf16[256,802]{0,1:T(8,128)(2,1)}, bf16[256,802]{0,1:T(8,128)(2,1)S(1)}, u32[]{:S(2)}, u32[]{:S(2)}) collective-permute-start(bf16[256,802]{0,1:T(8,128)(2,1)} %get-tuple-element.111), channel_id=1, source_target_pairs={{0,2},{1,3},{2,0},{3,1},{4,6},{5,7},{6,4},{7,5},{8,10},{9,11},{10,... | collective-permute-start | bytes 1231880 | tf_op jit(solution)/shard_map/ppermute | solution.py:45
  31.3 1.8 collective-permute-start.2
  31.6 14.5 %collective-permute-start.7 = (bf16[256,1024]{1,0:T(8,128)(2,1)}, bf16[256,1024]{1,0:T(8,128)(2,1)}, u32[]{:S(2)}, u32[]{:S(2)}) collective-permute-start(bf16[256,1024]{1,0:T(8,128)(2,1)} %collective-permute-done.6), channel_id=1, source_target_pairs={{0,1},{1,0},{2,3},{3,2},{4,5},{5,4},{6,7},{7,6},{8,9},{9,8},{10,11... | collective-permute-start | bytes 1572872 | tf_op jit(solution)/shard_map/ppermute | solution.py:45
  36.6 9.5 %copy-start.29 = (bf16[256,1024]{1,0:T(8,128)(2,1)S(1)}, bf16[256,1024]{1,0:T(8,128)(2,1)}, u32[]{:S(2)}) copy-start(bf16[256,1024]{1,0:T(8,128)(2,1)} %param.14) | copy-start | bytes 1572868
  36.8 9.1 %collective-permute-start.3 = (bf16[320,384]{1,0:T(8,128)(2,1)S(1)}, bf16[320,384]{1,0:T(8,128)(2,1)S(1)}, u32[]{:S(2)}, u32[]{:S(2)}) collective-permute-start(bf16[320,384]{1,0:T(8,128)(2,1)S(1)} %pad_maximum_fusion.24), channel_id=1, source_target_pairs={{0,2},{1,3},{4,6},{5,7},{8,10},{9,11},{12,14},{13,15},{16,18},{17,... | collective-permute-start | bytes 737288 | tf_op jit(solution)/shard_map/ppermute | solution.py:374
  46.0 3.1 collective-permute-start.4
  78.7 172.8 %copy-start.2 = (f32[384,1024]{1,0:T(8,128)}, f32[384,1024]{1,0:T(8,128)S(1)}, u32[]{:S(2)}) copy-start(f32[384,1024]{1,0:T(8,128)S(1)} %get-tuple-element.122) | copy-start | bytes 4718596
  80.1 36.6 %collective-permute-start.9 = (bf16[384,1024]{1,0:T(8,128)(2,1)}, bf16[384,1024]{1,0:T(8,128)(2,1)}, u32[]{:S(2)}, u32[]{:S(2)}) collective-permute-start(bf16[384,1024]{1,0:T(8,128)(2,1)} %multiply_convert_fusion.3), channel_id=1, source_target_pairs={{0,2},{1,3},{2,0},{3,1},{4,6},{5,7},{6,4},{7,5},{8,10},{9,11},{10,... | collective-permute-start | bytes 2359304 | tf_op jit(solution)/shard_map/ppermute | solution.py:45
  87.4 21.2 %collective-permute-start.13 = (bf16[256,704]{0,1:T(8,128)(2,1)}, bf16[256,704]{0,1:T(8,128)(2,1)}, u32[]{:S(2)}, u32[]{:S(2)}) collective-permute-start(bf16[256,704]{0,1:T(8,128)(2,1)} %get-tuple-element.88), channel_id=1, source_target_pairs={{0,3},{1,2},{2,1},{3,0},{4,7},{5,6},{6,5},{7,4},{8,11},{9,10},{10,... | collective-permute-start | bytes 1081352 | tf_op jit(solution)/shard_map/ppermute | solution.py:45
  87.5 29.2 %collective-permute-start.12 = (bf16[256,704]{0,1:T(8,128)(2,1)}, bf16[256,704]{0,1:T(8,128)(2,1)}, u32[]{:S(2)}, u32[]{:S(2)}) collective-permute-start(bf16[256,704]{0,1:T(8,128)(2,1)} %get-tuple-element.89), channel_id=1, source_target_pairs={{0,2},{1,3},{2,0},{3,1},{4,6},{5,7},{6,4},{7,5},{8,10},{9,11},{10,... | collective-permute-start | bytes 1081352 | tf_op jit(solution)/shard_map/ppermute | solution.py:45
  89.2 28.0 %collective-permute-start.11 = (bf16[256,704]{0,1:T(8,128)(2,1)}, bf16[256,704]{0,1:T(8,128)(2,1)}, u32[]{:S(2)}, u32[]{:S(2)}) collective-permute-start(bf16[256,704]{0,1:T(8,128)(2,1)} %get-tuple-element.90), channel_id=1, source_target_pairs={{0,1},{1,0},{2,3},{3,2},{4,5},{5,4},{6,7},{7,6},{8,9},{9,8},{10,11... | collective-permute-start | bytes 1081352 | tf_op jit(solution)/shard_map/ppermute | solution.py:45
  91.8 16.8 %copy-start.23 = (bf16[1,384,1024]{2,1,0:T(8,128)(2,1)S(1)}, bf16[1,384,1024]{2,1,0:T(8,128)(2,1)}, u32[]{:S(2)}) copy-start(bf16[1,384,1024]{2,1,0:T(8,128)(2,1)} %param.19) | copy-start | bytes 2359300
  93.3 30.6 %collective-permute-start.16 = (bf16[256,704]{0,1:T(8,128)(2,1)S(1)}, bf16[256,704]{0,1:T(8,128)(2,1)S(1)}, u32[]{:S(2)}, u32[]{:S(2)}) collective-permute-start(bf16[256,704]{0,1:T(8,128)(2,1)S(1)} %get-tuple-element.96), channel_id=1, source_target_pairs={{0,3},{1,2},{2,1},{3,0},{4,7},{5,6},{6,5},{7,4},{8,11},{9,10},{10,... | collective-permute-start | bytes 1081352 | tf_op jit(solution)/shard_map/ppermute | solution.py:45
  108.6 40.5 %collective-permute-start.21 = (bf16[384,1024]{1,0:T(8,128)(2,1)S(1)}, bf16[384,1024]{1,0:T(8,128)(2,1)S(1)}, u32[]{:S(2)}, u32[]{:S(2)}) collective-permute-start(bf16[384,1024]{1,0:T(8,128)(2,1)S(1)} %bitcast.240), channel_id=1, source_target_pairs={{0,2},{1,3},{2,0},{3,1},{4,6},{5,7},{6,4},{7,5},{8,10},{9,11},{10,... | collective-permute-start | bytes 2359304 | tf_op jit(solution)/shard_map/ppermute | solution.py:45
  116.7 32.9 %collective-permute-start.8 = (bf16[384,1024]{1,0:T(8,128)(2,1)}, bf16[384,1024]{1,0:T(8,128)(2,1)S(1)}, u32[]{:S(2)}, u32[]{:S(2)}) collective-permute-start(bf16[384,1024]{1,0:T(8,128)(2,1)} %multiply_convert_fusion.3), channel_id=1, source_target_pairs={{0,1},{1,0},{2,3},{3,2},{4,5},{5,4},{6,7},{7,6},{8,9},{9,8},{10,11... | collective-permute-start | bytes 2359304 | tf_op jit(solution)/shard_map/ppermute | solution.py:45
  116.7 32.9 %collective-permute-start.10 = (bf16[384,1024]{1,0:T(8,128)(2,1)}, bf16[384,1024]{1,0:T(8,128)(2,1)S(1)}, u32[]{:S(2)}, u32[]{:S(2)}) collective-permute-start(bf16[384,1024]{1,0:T(8,128)(2,1)} %collective-permute-done.9), channel_id=1, source_target_pairs={{0,1},{1,0},{2,3},{3,2},{4,5},{5,4},{6,7},{7,6},{8,9},{9,8},{10,11... | collective-permute-start | bytes 2359304 | tf_op jit(solution)/shard_map/ppermute | solution.py:45
  117.2 31.5 %collective-permute-start.15 = (bf16[256,704]{0,1:T(8,128)(2,1)S(1)}, bf16[256,704]{0,1:T(8,128)(2,1)S(1)}, u32[]{:S(2)}, u32[]{:S(2)}) collective-permute-start(bf16[256,704]{0,1:T(8,128)(2,1)S(1)} %get-tuple-element.97), channel_id=1, source_target_pairs={{0,2},{1,3},{2,0},{3,1},{4,6},{5,7},{6,4},{7,5},{8,10},{9,11},{10,... | collective-permute-start | bytes 1081352 | tf_op jit(solution)/shard_map/ppermute | solution.py:45
  123.9 24.8 %collective-permute-start.14 = (bf16[256,704]{0,1:T(8,128)(2,1)S(1)}, bf16[256,704]{0,1:T(8,128)(2,1)S(1)}, u32[]{:S(2)}, u32[]{:S(2)}) collective-permute-start(bf16[256,704]{0,1:T(8,128)(2,1)S(1)} %get-tuple-element.98), channel_id=1, source_target_pairs={{0,1},{1,0},{2,3},{3,2},{4,5},{5,4},{6,7},{7,6},{8,9},{9,8},{10,11... | collective-permute-start | bytes 1081352 | tf_op jit(solution)/shard_map/ppermute | solution.py:45
  148.7 9.2 %collective-permute-start.20 = (bf16[384,1024]{1,0:T(8,128)(2,1)S(1)}, bf16[384,1024]{1,0:T(8,128)(2,1)S(1)}, u32[]{:S(2)}, u32[]{:S(2)}) collective-permute-start(bf16[384,1024]{1,0:T(8,128)(2,1)S(1)} %bitcast.241), channel_id=1, source_target_pairs={{0,1},{1,0},{2,3},{3,2},{4,5},{5,4},{6,7},{7,6},{8,9},{9,8},{10,11... | collective-permute-start | bytes 2359304 | tf_op jit(solution)/shard_map/ppermute | solution.py:45
  149.1 8.9 %copy-start.35 = (bf16[384,1024]{1,0:T(8,128)(2,1)}, bf16[384,1024]{1,0:T(8,128)(2,1)S(1)}, u32[]{:S(2)}) copy-start(bf16[384,1024]{1,0:T(8,128)(2,1)S(1)} %collective-permute-done.21) | copy-start | bytes 2359300
  149.1 8.8 %collective-permute-start.22 = (bf16[384,1024]{1,0:T(8,128)(2,1)S(1)}, bf16[384,1024]{1,0:T(8,128)(2,1)S(1)}, u32[]{:S(2)}, u32[]{:S(2)}) collective-permute-start(bf16[384,1024]{1,0:T(8,128)(2,1)S(1)} %collective-permute-done.21), channel_id=1, source_target_pairs={{0,1},{1,0},{2,3},{3,2},{4,5},{5,4},{6,7},{7,6},{8,9},{9,8},{10,11... | collective-permute-start | bytes 2359304 | tf_op jit(solution)/shard_map/ppermute | solution.py:45
  149.6 23.5 %copy-start.41 = (bf16[384,1024]{1,0:T(8,128)(2,1)}, bf16[384,1024]{1,0:T(8,128)(2,1)S(1)}, u32[]{:S(2)}) copy-start(bf16[384,1024]{1,0:T(8,128)(2,1)S(1)} %collective-permute-done.8) | copy-start | bytes 2359300
  149.6 23.5 %copy-start.42 = (bf16[384,1024]{1,0:T(8,128)(2,1)}, bf16[384,1024]{1,0:T(8,128)(2,1)S(1)}, u32[]{:S(2)}) copy-start(bf16[384,1024]{1,0:T(8,128)(2,1)S(1)} %collective-permute-done.10) | copy-start | bytes 2359300
  157.9 10.0 %copy-start.37 = (bf16[384,1024]{1,0:T(8,128)(2,1)}, bf16[384,1024]{1,0:T(8,128)(2,1)S(1)}, u32[]{:S(2)}) copy-start(bf16[384,1024]{1,0:T(8,128)(2,1)S(1)} %collective-permute-done.20) | copy-start | bytes 2359300
  157.9 10.0 %copy-start.39 = (bf16[384,1024]{1,0:T(8,128)(2,1)}, bf16[384,1024]{1,0:T(8,128)(2,1)S(1)}, u32[]{:S(2)}) copy-start(bf16[384,1024]{1,0:T(8,128)(2,1)S(1)} %collective-permute-done.22) | copy-start | bytes 2359300
  192.1 13.6 %slice-start = ((s8[6291456]{0:T(1024)(128)(4,1)}), s8[4194304]{0:T(1024)(128)(4,1)S(1)}, s32[]{:S(2)}) async-start(s8[6291456]{0:T(1024)(128)(4,1)} %bitcast.227), calls=%async_computation.1 | async-start | bytes 8388608
  198.6 7.1 %slice-start.1 = ((s8[6291456]{0:T(1024)(128)(4,1)}), s8[2097152]{0:T(1024)(128)(4,1)S(1)}, s32[]{:S(2)}) async-start(s8[6291456]{0:T(1024)(128)(4,1)} %bitcast.227), calls=%async_computation.2 | async-start | bytes 4194304
  198.7 15.1 %collective-permute-start.45 = (bf16[256,704]{0,1:T(8,128)(2,1)S(1)}, bf16[256,704]{0,1:T(8,128)(2,1)S(1)}, u32[]{:S(2)}, u32[]{:S(2)}) collective-permute-start(bf16[256,704]{0,1:T(8,128)(2,1)S(1)} %bitcast.261), channel_id=1, source_target_pairs={{0,3},{1,2},{2,1},{3,0},{4,7},{5,6},{6,5},{7,4},{8,11},{9,10},{10,... | collective-permute-start | bytes 1081352 | tf_op jit(solution)/shard_map/ppermute | solution.py:45
  200.7 13.4 %collective-permute-start.43 = (bf16[256,704]{0,1:T(8,128)(2,1)S(1)}, bf16[256,704]{0,1:T(8,128)(2,1)S(1)}, u32[]{:S(2)}, u32[]{:S(2)}) collective-permute-start(bf16[256,704]{0,1:T(8,128)(2,1)S(1)} %bitcast.259), channel_id=1, source_target_pairs={{0,1},{1,0},{2,3},{3,2},{4,5},{5,4},{6,7},{7,6},{8,9},{9,8},{10,11... | collective-permute-start | bytes 1081352 | tf_op jit(solution)/shard_map/ppermute | solution.py:45
  200.7 17.2 %collective-permute-start.44 = (bf16[256,704]{0,1:T(8,128)(2,1)S(1)}, bf16[256,704]{0,1:T(8,128)(2,1)S(1)}, u32[]{:S(2)}, u32[]{:S(2)}) collective-permute-start(bf16[256,704]{0,1:T(8,128)(2,1)S(1)} %bitcast.258), channel_id=1, source_target_pairs={{0,2},{1,3},{2,0},{3,1},{4,6},{5,7},{6,4},{7,5},{8,10},{9,11},{10,... | collective-permute-start | bytes 1081352 | tf_op jit(solution)/shard_map/ppermute | solution.py:45
  204.2 20.7 %collective-permute-start.42 = (bf16[256,704]{0,1:T(8,128)(2,1)S(1)}, bf16[256,704]{0,1:T(8,128)(2,1)S(1)}, u32[]{:S(2)}, u32[]{:S(2)}) collective-permute-start(bf16[256,704]{0,1:T(8,128)(2,1)S(1)} %bitcast.257), channel_id=1, source_target_pairs={{0,3},{1,2},{2,1},{3,0},{4,7},{5,6},{6,5},{7,4},{8,11},{9,10},{10,... | collective-permute-start | bytes 1081352 | tf_op jit(solution)/shard_map/ppermute | solution.py:45
  208.6 4.6 collective-permute-start.24
  213.0 6.6 %copy-start.24 = (bf16[1,384,1024]{2,1,0:T(8,128)(2,1)S(1)}, bf16[1,384,1024]{2,1,0:T(8,128)(2,1)}, u32[]{:S(2)}) copy-start(bf16[1,384,1024]{2,1,0:T(8,128)(2,1)} %param.19) | copy-start | bytes 2359300
  213.1 10.2 %collective-permute-start.18 = (bf16[384,1024]{1,0:T(8,128)(2,1)S(1)}, bf16[384,1024]{1,0:T(8,128)(2,1)S(1)}, u32[]{:S(2)}, u32[]{:S(2)}) collective-permute-start(bf16[384,1024]{1,0:T(8,128)(2,1)S(1)} %get-tuple-element.54), channel_id=1, source_target_pairs={{0,1},{1,0},{2,3},{3,2},{4,5},{5,4},{6,7},{7,6},{8,9},{9,8},{10,11... | collective-permute-start | bytes 2359304 | tf_op jit(solution)/shard_map/ppermute | solution.py:45
  213.8 11.7 %collective-permute-start.40 = (bf16[256,704]{0,1:T(8,128)(2,1)S(1)}, bf16[256,704]{0,1:T(8,128)(2,1)S(1)}, u32[]{:S(2)}, u32[]{:S(2)}) collective-permute-start(bf16[256,704]{0,1:T(8,128)(2,1)S(1)} %bitcast.260), channel_id=1, source_target_pairs={{0,1},{1,0},{2,3},{3,2},{4,5},{5,4},{6,7},{7,6},{8,9},{9,8},{10,11... | collective-permute-start | bytes 1081352 | tf_op jit(solution)/shard_map/ppermute | solution.py:45
  214.1 37.4 %collective-permute-start.23 = (bf16[384,1024]{1,0:T(8,128)(2,1)S(1)}, bf16[384,1024]{1,0:T(8,128)(2,1)S(1)}, u32[]{:S(2)}, u32[]{:S(2)}) collective-permute-start(bf16[384,1024]{1,0:T(8,128)(2,1)S(1)} %get-tuple-element.51), channel_id=1, source_target_pairs={{0,1},{1,0},{2,3},{3,2},{4,5},{5,4},{6,7},{7,6},{8,9},{9,8},{10,11... | collective-permute-start | bytes 2359304 | tf_op jit(solution)/shard_map/ppermute | solution.py:45
  217.9 33.6 %collective-permute-start.25 = (bf16[384,1024]{1,0:T(8,128)(2,1)S(1)}, bf16[384,1024]{1,0:T(8,128)(2,1)S(1)}, u32[]{:S(2)}, u32[]{:S(2)}) collective-permute-start(bf16[384,1024]{1,0:T(8,128)(2,1)S(1)} %fusion.12), channel_id=1, source_target_pairs={{0,2},{1,3},{2,0},{3,1},{4,6},{5,7},{6,4},{7,5},{8,10},{9,11},{10,... | collective-permute-start | bytes 2359304 | tf_op jit(solution)/shard_map/ppermute | solution.py:45
  223.4 26.8 %collective-permute-start.41 = (bf16[256,704]{0,1:T(8,128)(2,1)S(1)}, bf16[256,704]{0,1:T(8,128)(2,1)S(1)}, u32[]{:S(2)}, u32[]{:S(2)}) collective-permute-start(bf16[256,704]{0,1:T(8,128)(2,1)S(1)} %bitcast.262), channel_id=1, source_target_pairs={{0,2},{1,3},{2,0},{3,1},{4,6},{5,7},{6,4},{7,5},{8,10},{9,11},{10,... | collective-permute-start | bytes 1081352 | tf_op jit(solution)/shard_map/ppermute | solution.py:45
  224.9 27.3 %collective-permute-start.17 = (bf16[384,1024]{1,0:T(8,128)(2,1)S(1)}, bf16[384,1024]{1,0:T(8,128)(2,1)S(1)}, u32[]{:S(2)}, u32[]{:S(2)}) collective-permute-start(bf16[384,1024]{1,0:T(8,128)(2,1)S(1)} %get-tuple-element.53), channel_id=1, source_target_pairs={{0,1},{1,0},{2,3},{3,2},{4,5},{5,4},{6,7},{7,6},{8,9},{9,8},{10,11... | collective-permute-start | bytes 2359304 | tf_op jit(solution)/shard_map/ppermute | solution.py:45
  225.5 41.0 %collective-permute-start.19 = (bf16[384,1024]{1,0:T(8,128)(2,1)S(1)}, bf16[384,1024]{1,0:T(8,128)(2,1)S(1)}, u32[]{:S(2)}, u32[]{:S(2)}) collective-permute-start(bf16[384,1024]{1,0:T(8,128)(2,1)S(1)} %fusion.14), channel_id=1, source_target_pairs={{0,2},{1,3},{2,0},{3,1},{4,6},{5,7},{6,4},{7,5},{8,10},{9,11},{10,... | collective-permute-start | bytes 2359304 | tf_op jit(solution)/shard_map/ppermute | solution.py:45
  252.2 17.6 %copy-start.30 = (bf16[256,1024]{1,0:T(8,128)(2,1)S(1)}, bf16[256,1024]{1,0:T(8,128)(2,1)}, u32[]{:S(2)}) copy-start(bf16[256,1024]{1,0:T(8,128)(2,1)} %get-tuple-element.55) | copy-start | bytes 1572868
  252.2 17.5 %copy-start.31 = (bf16[256,1024]{1,0:T(8,128)(2,1)S(1)}, bf16[256,1024]{1,0:T(8,128)(2,1)}, u32[]{:S(2)}) copy-start(bf16[256,1024]{1,0:T(8,128)(2,1)} %get-tuple-element.56) | copy-start | bytes 1572868
  252.2 17.5 %copy-start.32 = (bf16[256,1024]{1,0:T(8,128)(2,1)S(1)}, bf16[256,1024]{1,0:T(8,128)(2,1)}, u32[]{:S(2)}) copy-start(bf16[256,1024]{1,0:T(8,128)(2,1)} %get-tuple-element.57) | copy-start | bytes 1572868
  252.2 17.5 %copy-start.33 = (bf16[256,1024]{1,0:T(8,128)(2,1)S(1)}, bf16[256,1024]{1,0:T(8,128)(2,1)}, u32[]{:S(2)}) copy-start(bf16[256,1024]{1,0:T(8,128)(2,1)} %get-tuple-element.58) | copy-start | bytes 1572868
  308.7 5.2 collective-permute-start.26
  311.7 21.6 %collective-permute-start.37 = (bf16[256,1024]{1,0:T(8,128)(2,1)}, bf16[256,1024]{1,0:T(8,128)(2,1)}, u32[]{:S(2)}, u32[]{:S(2)}) collective-permute-start(bf16[256,1024]{1,0:T(8,128)(2,1)} %get-tuple-element.47), channel_id=1, source_target_pairs={{0,1},{1,0},{2,3},{3,2},{4,5},{5,4},{6,7},{7,6},{8,9},{9,8},{10,11... | collective-permute-start | bytes 1572872 | tf_op jit(solution)/shard_map/ppermute | solution.py:45
  312.2 13.3 %collective-permute-start.38 = (bf16[256,1024]{1,0:T(8,128)(2,1)}, bf16[256,1024]{1,0:T(8,128)(2,1)S(1)}, u32[]{:S(2)}, u32[]{:S(2)}) collective-permute-start(bf16[256,1024]{1,0:T(8,128)(2,1)} %get-tuple-element.48), channel_id=1, source_target_pairs={{0,1},{1,0},{2,3},{3,2},{4,5},{5,4},{6,7},{7,6},{8,9},{9,8},{10,11... | collective-permute-start | bytes 1572872 | tf_op jit(solution)/shard_map/ppermute | solution.py:45
  314.0 10.2 %collective-permute-start.27 = (bf16[320,384]{1,0:T(8,128)(2,1)S(1)}, bf16[320,384]{1,0:T(8,128)(2,1)S(1)}, u32[]{:S(2)}, u32[]{:S(2)}) collective-permute-start(bf16[320,384]{1,0:T(8,128)(2,1)S(1)} %fusion.40), channel_id=1, source_target_pairs={{2,0},{3,1},{6,4},{7,5},{10,8},{11,9},{14,12},{15,13},{18,16},{19,... | collective-permute-start | bytes 737288 | tf_op jit(solution)/shard_map/ppermute | solution.py:463
  327.3 13.5 %collective-permute-start.39 = (bf16[256,1024]{1,0:T(8,128)(2,1)S(1)}, bf16[256,1024]{1,0:T(8,128)(2,1)S(1)}, u32[]{:S(2)}, u32[]{:S(2)}) collective-permute-start(bf16[256,1024]{1,0:T(8,128)(2,1)S(1)} %fusion.22), channel_id=1, source_target_pairs={{0,2},{1,3},{2,0},{3,1},{4,6},{5,7},{6,4},{7,5},{8,10},{9,11},{10,... | collective-permute-start | bytes 1572872 | tf_op jit(solution)/shard_map/ppermute | solution.py:45
  346.8 1.8 collective-permute-start.29
  346.9 2.5 collective-permute-start.28
  348.7 11.8 %collective-permute-start.30 = (bf16[256,802]{0,1:T(8,128)(2,1)S(1)}, bf16[256,802]{0,1:T(8,128)(2,1)}, u32[]{:S(2)}, u32[]{:S(2)}) collective-permute-start(bf16[256,802]{0,1:T(8,128)(2,1)S(1)} %fusion.25), channel_id=1, source_target_pairs={{0,2},{1,3},{2,0},{3,1},{4,6},{5,7},{6,4},{7,5},{8,10},{9,11},{10,... | collective-permute-start | bytes 1231880 | tf_op jit(solution)/shard_map/ppermute | solution.py:45
  362.1 10.8 %collective-permute-start.31 = (bf16[128,802]{0,1:T(8,128)(2,1)S(1)}, bf16[128,802]{0,1:T(8,128)(2,1)S(1)}, u32[]{:S(2)}, u32[]{:S(2)}) collective-permute-start(bf16[128,802]{0,1:T(8,128)(2,1)S(1)} %broadcast_select_fusion.1), channel_id=1, source_target_pairs={{0,4},{4,0},{8,12},{12,8},{16,20},{20,16},{24,28},{28,24},{1,5},{5... | collective-permute-start | bytes 615944 | tf_op jit(solution)/shard_map/ppermute | solution.py:45
  373.1 24.2 %collective-permute-start.32 = (bf16[64,802]{0,1:T(8,128)(2,1)S(1)}, bf16[64,802]{0,1:T(8,128)(2,1)S(1)}, u32[]{:S(2)}, u32[]{:S(2)}) collective-permute-start(bf16[64,802]{0,1:T(8,128)(2,1)S(1)} %broadcast_select_fusion.2), channel_id=1, source_target_pairs={{0,8},{4,12},{8,0},{12,4},{16,24},{20,28},{24,16},{28,20},{1,9},{5... | collective-permute-start | bytes 307976 | tf_op jit(solution)/shard_map/ppermute | solution.py:45
  374.7 70.2 %copy-start.8 = (f32[384,1024]{1,0:T(8,128)S(1)}, f32[384,1024]{1,0:T(8,128)}, u32[]{:S(2)}) copy-start(f32[384,1024]{1,0:T(8,128)} %copy-done.7) | copy-start | bytes 4718596
  397.6 16.7 %collective-permute-start.33 = (bf16[32,802]{0,1:T(8,128)(2,1)S(1)}, bf16[32,802]{0,1:T(8,128)(2,1)S(1)}, u32[]{:S(2)}, u32[]{:S(2)}) collective-permute-start(bf16[32,802]{0,1:T(8,128)(2,1)S(1)} %broadcast_select_fusion.3), channel_id=1, source_target_pairs={{0,16},{4,20},{8,24},{12,28},{16,0},{20,4},{24,8},{28,12},{1,17},{... | collective-permute-start | bytes 153992 | tf_op jit(solution)/shard_map/ppermute | solution.py:45
  414.5 17.3 %collective-permute-start.34 = (bf16[32,802]{0,1:T(8,128)(2,1)S(1)}, bf16[32,802]{0,1:T(8,128)(2,1)S(1)}, u32[]{:S(2)}, u32[]{:S(2)}) collective-permute-start(bf16[32,802]{0,1:T(8,128)(2,1)S(1)} %add_convert_fusion), channel_id=1, source_target_pairs={{0,16},{4,20},{8,24},{12,28},{16,0},{20,4},{24,8},{28,12},{1,17},{... | collective-permute-start | bytes 153992 | tf_op jit(solution)/shard_map/ppermute | solution.py:45
  432.0 10.9 %collective-permute-start.35 = (bf16[64,802]{0,1:T(8,128)(2,1)S(1)}, bf16[64,802]{0,1:T(8,128)(2,1)S(1)}, u32[]{:S(2)}, u32[]{:S(2)}) collective-permute-start(bf16[64,802]{0,1:T(8,128)(2,1)S(1)} %maximum_select_fusion.1), channel_id=1, source_target_pairs={{0,8},{4,12},{8,0},{12,4},{16,24},{20,28},{24,16},{28,20},{1,9},{5... | collective-permute-start | bytes 307976 | tf_op jit(solution)/shard_map/ppermute | solution.py:45
  443.1 7.0 %collective-permute-start.36 = (bf16[128,802]{0,1:T(8,128)(2,1)S(1)}, bf16[128,802]{0,1:T(8,128)(2,1)S(1)}, u32[]{:S(2)}, u32[]{:S(2)}) collective-permute-start(bf16[128,802]{0,1:T(8,128)(2,1)S(1)} %maximum_select_fusion.2), channel_id=1, source_target_pairs={{0,4},{4,0},{8,12},{12,8},{16,20},{20,16},{24,28},{28,24},{1,5},{5... | collective-permute-start | bytes 615944 | tf_op jit(solution)/shard_map/ppermute | solution.py:45
  (29 other events, 95.5 us)
Sparse Core Ops, SparseCore 0:
  343.3 186.1 all-reduce.2
